TPU v7x, 128 devices: a whole 4x4x4 slice. The times are simulated.
128 devices in a mesh: alpha: 16 (over x_lo, z, core), beta: 8 (over x_hi, y).
Axes of the slice: x: 4 (x_hi: 2, x_lo: 2; x = x_hi * 2 + x_lo), y: 4, z: 4, core: 2. Of those that a mesh axis runs over, the one named last changes fastest.
Arguments:
- coefficients: bfloat16 [8192, 8192], P('alpha', 'beta'), may hold values from -6 to 6
- diagonal: float32 [8192, 8192], P('alpha', 'beta'), may hold values from 0.5 to 2
- alpha_blocks: bfloat16 [64, 14, 128, 128], P('alpha'), may hold values from -0.125 to 0.125
- alpha_lists: int32 [64, 14], replicated, may hold values from 0 to 63, as said below
- beta_blocks: bfloat16 [64, 14, 128, 128], P('beta'), may hold values from -0.125 to 0.125
- beta_lists: int32 [64, 14], replicated, may hold values from 0 to 63, as said below
Outputs:
- sigma_out: bfloat16 [8192, 8192], P('alpha', 'beta')
Inputs may be any that keep to these rules, and one draw needn't show every extreme that they name: `alpha_lists`: each row names 14 different blocks. For every alpha device, the rows of its 4 block rows name at most 2 different blocks owned by any one alpha device (blocks j * 4 to (j + 1) * 4 - 1 belong to device j), and exactly 2 from some owner. `beta_lists`: each row names 14 different blocks. For every beta device, the rows of its 8 block rows name at most 4 different blocks owned by any one beta device (blocks j * 8 to (j + 1) * 8 - 1 belong to device j), and exactly 4 from some owner.
All inputs are finite; a program needn't handle non-finite values.
Results may differ from a plain program's by a relative error of at most 0.001.
Values may be sent and summed in bfloat16 or wider, within the bound.
A program may use at most 128 MiB of HBM per device.

v0:
```python
import jax
import jax.numpy as jnp
from jax import lax
from jax.sharding import PartitionSpec as P

CAP_B = 4


def piece_weights(list_ids, number, blocks_here):
    hits = (list_ids[:, :, None] == jnp.arange(number, dtype=jnp.int32)).astype(jnp.bfloat16)
    combined = jnp.einsum("rkj,rkab->rjab", hits, blocks_here, preferred_element_type=jnp.float32)
    return combined.astype(jnp.bfloat16)


def wanted(columns, first_id, number):
    targets = first_id + jnp.arange(number, dtype=jnp.int32)
    return jnp.any(columns[..., :, None] == targets, axis=-2)


def slot_onehot(needed, limit):
    position = jnp.cumsum(needed.astype(jnp.int32), axis=-1) - 1
    hits = needed[..., None] & (position[..., None] == jnp.arange(limit, dtype=jnp.int32))
    return hits.astype(jnp.bfloat16)


def slot_index(list_ids, owners, per_owner, limit):
    needed = wanted(list_ids.reshape(1, -1), 0, owners * per_owner)[0]
    position = jnp.cumsum(needed.reshape(owners, per_owner).astype(jnp.int32), axis=-1) - 1
    return list_ids // per_owner * limit + jnp.take(position.reshape(-1), list_ids)


def per_device(coefficients, diagonal, alpha_blocks, alpha_lists, beta_blocks, beta_lists):
    block = alpha_blocks.shape[2]
    rows_a = alpha_blocks.shape[0]
    rows_b = beta_blocks.shape[0]
    height = coefficients.shape[0]
    columns_dev = coefficients.shape[1]
    owners_b = lax.axis_size("beta")
    index_a = lax.axis_index("alpha")
    index_b = lax.axis_index("beta")
    mine_a = lax.dynamic_slice_in_dim(alpha_lists, index_a * rows_a, rows_a, 0)
    mine_b = lax.dynamic_slice_in_dim(beta_lists, index_b * rows_b, rows_b, 0)
    piece_rows = lax.all_gather(coefficients, "alpha", axis=0, tiled=True)
    number = piece_rows.shape[0] // block
    combined = piece_weights(mine_a, number, alpha_blocks)
    piece_blocks = piece_rows.reshape(number, block, columns_dev)
    alpha_term = jnp.einsum(
        "rjab,jbn->ran", combined, piece_blocks, preferred_element_type=jnp.float32
    ).reshape(height, columns_dev)
    needed_b = wanted(
        beta_lists.reshape(owners_b, rows_b * beta_blocks.shape[1]), index_b * rows_b, rows_b
    )
    onehot_b = slot_onehot(needed_b, CAP_B)
    outgoing_b = jnp.einsum(
        "djc,mjb->dcmb",
        onehot_b,
        coefficients.reshape(height, rows_b, block),
        preferred_element_type=jnp.float32,
    ).astype(jnp.bfloat16)
    arrived_b = lax.all_to_all(outgoing_b, "beta", split_axis=0, concat_axis=0, tiled=True)
    slot_ids_b = slot_index(mine_b, owners_b, rows_b, CAP_B)
    chosen_b = jnp.take(arrived_b.reshape(owners_b * CAP_B, height, block), slot_ids_b, axis=0)
    beta_term = jnp.einsum(
        "rkmb,rkab->mra", chosen_b, beta_blocks, preferred_element_type=jnp.float32
    ).reshape(height, columns_dev)
    sigma_out = alpha_term + beta_term + diagonal * coefficients.astype(jnp.float32)
    return sigma_out.astype(jnp.bfloat16)


def solution(mesh):
    in_specs = (
        P("alpha", "beta"),
        P("alpha", "beta"),
        P("alpha", None, None, None),
        P(),
        P("beta", None, None, None),
        P(),
    )
    out_specs = P("alpha", "beta")
    return jax.shard_map(
        per_device, mesh=mesh, in_specs=in_specs, out_specs=out_specs, check_vma=False
    )
```

profile of v0, /device:TPU:1, one launch (start us, length us, event | category | flops | bytes accessed | tf_op | source)
XLA Modules:
  0.0 181.0 jit_solution(18134677144941743787)
XLA Ops:
  6.5 0.0 copy-start
  6.5 0.0 all-gather.2.cloned.1.call-start
  6.5 0.7 all-gather.2.cloned.1.call-update
  7.3 0.8 copy.29
  8.0 0.1 eq.71
  8.1 0.3 compare_reduce_fusion
  8.4 1.5 copy.37
  9.9 0.2 reduce_window_sum.18
  10.1 1.2 convolution_convert_fusion.1
  11.3 2.9 %copy.31 = bf16[8,4,512,128]{3,2,1,0:T(8,128)(2,1)} copy(bf16[8,4,512,128]{3,0,2,1:T(8,128)(2,1)S(1)} %convolution_convert_fusion.1) | data formatting | bytes 8388608 | tf_op jit(solution)/shard_map/convert_element_type | solution.py:59
  14.2 7.5 %all-to-all-start = ((bf16[8,4,512,128]{3,2,1,0:T(8,128)(2,1)}), bf16[8,4,512,128]{3,2,1,0:T(8,128)(2,1)}, u32[]{:S(2)}, u32[]{:S(2)}) async-start(bf16[8,4,512,128]{3,2,1,0:T(8,128)(2,1)} %copy.31), calls=%async_computation | async-start | bytes 8388608 | tf_op jit(solution)/shard_map/all_to_all | solution.py:60
  21.7 0.0 copy-start.3
  21.7 0.1 eq.67
  21.8 0.1 fusion.13
  21.9 0.1 reshape.91
  22.0 0.2 reduce_window_sum.17
  22.2 0.1 sub.16
  22.3 0.1 reshape.94
  22.4 1.2 gather_fusion
  23.6 0.1 reshape.93
  23.7 0.1 reshape.102
  23.8 0.0 copy-done.3
  23.8 0.1 constant_dynamic-slice_fusion.1
  23.9 0.1 copy.26
  24.0 0.0 copy-done
  24.0 5.7 %convolution_convert_fusion = bf16[4,64,128,128]{3,1,2,0:T(8,128)(2,1)} fusion(bf16[4,14,128,128]{3,2,1,0:T(8,128)(2,1)S(1)} %copy-done, s32[4,14]{1,0:T(4,128)S(1)} %copy.26), kind=kOutput, calls=%fused_computation.8 | convolution fusion | flops 121638400 | bytes 10223840 | tf_op jit(solution)/shard_map/rkj,rkab->rjab/dot_general | solution.py:11
  29.7 85.8 %all-to-all-done = bf16[8,4,512,128]{3,2,1,0:T(8,128)(2,1)} async-done(((bf16[8,4,512,128]{3,2,1,0:T(8,128)(2,1)}), bf16[8,4,512,128]{3,2,1,0:T(8,128)(2,1)}, u32[]{:S(2)}, u32[]{:S(2)}) %all-to-all-start) | async-done | bytes 4194336 | tf_op jit(solution)/shard_map/all_to_all | solution.py:60
  115.5 10.1 %gather_fusion.1 = bf16[112,512,128]{2,1,0:T(8,128)(2,1)} fusion(bf16[32,512,128]{2,1,0:T(8,128)(2,1)} %bitcast.8, s32[1024]{0:T(1024)S(1)} %pad_clamp_fusion), kind=kCustom, calls=%fused_computation.1 | custom fusion | bytes 29360576 | tf_op jit(solution)/shard_map/jit(_take)/gather | solution.py:62
  125.6 10.6 %fusion = f32[8,512,128,1]{1,2,3,0:T(8,128)} fusion(bf16[8,14,128,128]{3,2,1,0:T(8,128)(2,1)} %param.10, bf16[8,14,512,128]{3,2,1,0:T(8,128)(2,1)} %bitcast.35, pred[8,14]{1,0:T(8,128)(4,1)S(1)} %get-tuple-element.5), kind=kOutput, calls=%fused_computation.2 | convolution fusion | flops 1886388224 | bytes 20447344 | tf_op jit(solution)/shard_map/rkmb,rkab->mra/dot_general | solution.py:63
  136.1 0.0 copy-start.2
  136.2 3.0 %copy.36 = f32[512,1024]{1,0:T(8,128)} copy(f32[512,1024]{0,1:T(8,128)} %bitcast.39) | data formatting | bytes 4194304 | tf_op jit(solution)/shard_map/reshape | solution.py:65
  139.2 9.7 %all-gather.2.cloned.1.call-done = bf16[8192,1024]{1,0:T(8,128)(2,1)} async-done(((bf16[512,1024]{1,0:T(8,128)(2,1)}), bf16[8192,1024]{1,0:T(8,128)(2,1)}) %all-gather.2.cloned.1.call-update) | async-done | bytes 16777232 | tf_op jit(solution)/shard_map/all_gather | solution.py:43
  148.9 0.0 copy-done.2
  148.9 0.0 copy-start.1
  148.9 25.2 %fusion.7 = bf16[512,1024]{1,0:T(8,128)(2,1)} fusion(f32[512,1024]{1,0:T(8,128)} %copy.36, f32[512,1024]{1,0:T(8,128)} %param.7, bf16[512,1024]{1,0:T(8,128)(2,1)S(1)} %copy-done.2, bf16[64,128,1024]{2,1,0:T(8,128)(2,1)} %bitcast.40, bf16[512,128,64]{1,2,0:T(8,128)(2,1)} %bitcast.36), kind=kOutput, calls=%fused_computation.12 | convolution fusion | flops 8592556032 | bytes 31457280 | tf_op jit(solution)/shard_map/rjab,jbn->ran/dot_general | solution.py:47
  174.1 0.0 copy-done.1
  (9 shorter events, 0.1 us)
Async XLA Ops:
  6.5 17.4 %copy-start = (bf16[4,14,128,128]{3,2,1,0:T(8,128)(2,1)S(1)}, bf16[4,14,128,128]{3,2,1,0:T(8,128)(2,1)}, u32[]{:S(2)}) copy-start(bf16[4,14,128,128]{3,2,1,0:T(8,128)(2,1)} %param.8) | copy-start | bytes 5505028
  6.5 142.3 %all-gather.2.cloned.1.call-start = ((), (), s32[]{:S(2)}) async-start(), calls=%async_computation.1 | async-start | bytes 17825792 | tf_op jit(solution)/shard_map/all_gather | solution.py:43
  14.2 101.2 %all-to-all-start = ((bf16[8,4,512,128]{3,2,1,0:T(8,128)(2,1)}), bf16[8,4,512,128]{3,2,1,0:T(8,128)(2,1)}, u32[]{:S(2)}, u32[]{:S(2)}) async-start(bf16[8,4,512,128]{3,2,1,0:T(8,128)(2,1)} %copy.31), calls=%async_computation | async-start | bytes 8388608 | tf_op jit(solution)/shard_map/all_to_all | solution.py:60
  21.7 2.1 %copy-start.3 = (s32[64,14]{0,1:T(8,128)S(1)}, s32[64,14]{0,1:T(8,128)}, u32[]{:S(2)}) copy-start(s32[64,14]{0,1:T(8,128)} %param.9) | copy-start | bytes 10756
  136.1 12.7 %copy-start.2 = (bf16[512,1024]{1,0:T(8,128)(2,1)S(1)}, bf16[512,1024]{1,0:T(8,128)(2,1)}, u32[]{:S(2)}) copy-start(bf16[512,1024]{1,0:T(8,128)(2,1)} %param.6) | copy-start | bytes 3145732
  148.9 25.2 %copy-start.1 = (bf16[4,14,128,128]{3,2,1,0:T(8,128)(2,1)S(1)}, bf16[4,14,128,128]{3,2,1,0:T(8,128)(2,1)}, u32[]{:S(2)}) copy-start(bf16[4,14,128,128]{3,2,1,0:T(8,128)(2,1)} %param.8) | copy-start | bytes 5505028
Sparse Core Ops, SparseCore 0:
  9.0 139.7 all-gather.1
where the time goes:
time: 181 us
  waiting for transfers between devices  96.2 us (53%)
  matrix products  42.8 us (24%)
  local copies, waits for them, and re-layouts  20.3 us (11%)
  between operations  13.5 us (7%)
  starting transfers between devices  7.47 us (4%)
    all_to_all x1, waiting for transfers between devices, per_device(): lax.all_to_all(outgoing_b, 'beta', split_axis=0, concat_axis=0, tiled=True)  85.8 us
    dot_general x1, matrix products, per_device(): jnp.einsum('rjab,jbn->ran', combined, piece_blocks, preferred_element_typ...  25.2 us
    dot_general x1, matrix products, per_device(): jnp.einsum('rkmb,rkab->mra', chosen_b, beta_blocks, preferred_element_typ...  10.6 us
    gather x1, local copies, waits for them, and re-layouts, per_device(): jnp.take(arrived_b.reshape(owners_b * CAP_B, height, block), slot_ids_b,...  10.1 us
    all_gather x1, waiting for transfers between devices, per_device(): piece_rows = lax.all_gather(coefficients, 'alpha', axis=0, tiled=True)  9.67 us
    all_to_all x1, starting transfers between devices, per_device(): lax.all_to_all(outgoing_b, 'beta', split_axis=0, concat_axis=0, tiled=True)  7.47 us
    dot_general x1, matrix products, piece_weights(): jnp.einsum('rkj,rkab->rjab', hits, blocks_here, preferred_element_type=jn...  5.71 us
  transfers between devices with their start and end apart: 2, of which 2 were waited for; matrix products, arithmetic and copies ran while one was open for 21% of the time, Pallas kernels for 0%

commit v1 on v0

v1 whole, which is shorter than its diff:
```python
import functools

import jax
import jax.numpy as jnp
from jax import lax
from jax.experimental import pallas as pl
from jax.experimental.pallas import tpu as pltpu
from jax.sharding import PartitionSpec as P

MESH = pl.DeviceIdType.MESH
BLK = 128
SLOTS = 14
RA = 4
RB = 8
CAP_A = 2
CAP_B = 4
ROWS = RA * BLK
COLS = RB * BLK

PIECES = {"n0": (0, 9), "n1": (9, 9), "f0": (18, 7), "f1": (25, 7)}
GROUPS = ROWS // 16
PER = BLK // 16
COMPUTE = True


def body(sel_a, inv_a, sel_b, inv_b, c_hbm, diag_hbm, ab_hbm, bb_hbm, out_ref, *scratch):
    it = iter(scratch)
    own, own_cb, peer_cb = next(it), next(it), next(it)
    gathered = {}
    for dx in range(2):
        for dz in range(4):
            for dc in range(2):
                if (dx, dz, dc) != (0, 0, 0):
                    gathered[dx, dz, dc] = next(it)
    peer = next(it)
    message = {(q, dy): next(it) for q in range(2) for dy in (1, 2, 3)}
    relay = {(q, up): next(it) for q in range(2) for up in range(2)}
    staged = {(q, dy): next(it) for q in range(2) for dy in (1, 2, 3)}
    ablk, bblk, diag, acc, wa, wb, xa, xb, send_sems, recv_sems, local_sems = it

    ia, ib = lax.axis_index("alpha"), lax.axis_index("beta")
    x_lo, z, core = ia // 8, (ia // 2) % 4, ia % 2
    x_hi, y = ib // 4, ib % 4

    def alpha_at(dx, dz, dc):
        return ((x_lo + dx) % 2) * 8 + ((z + dz) % 4) * 2 + (core + dc) % 2

    def beta_at(dxh, dy):
        return ((x_hi + dxh) % 2) * 4 + (y + dy) % 4

    target = {
        "s": (alpha_at(0, 0, 1), ib),
        "xi": (alpha_at(1, 0, 0), ib),
        "xo": (alpha_at(1, 0, 0), beta_at(1, 0)),
        "z+": (alpha_at(0, 1, 0), ib),
        "z-": (alpha_at(0, 3, 0), ib),
        "y+": (ia, beta_at(0, 1)),
        "y-": (ia, beta_at(0, 3)),
    }
    count = [0]
    started = []

    def send(link, src, dst):
        n = count[0]
        count[0] += 1
        copy = pltpu.make_async_remote_copy(
            src_ref=src,
            dst_ref=dst,
            send_sem=send_sems.at[n],
            recv_sem=recv_sems.at[n],
            device_id=target[link],
            device_id_type=MESH,
        )
        copy.start()
        started.append(copy)
        return copy

    def rows(ref, piece):
        first, size = PIECES[piece]
        return ref.at[pl.ds(first, size)]

    load_own = pltpu.make_async_copy(c_hbm, own, local_sems.at[0])
    load_own.start()
    load_a = pltpu.make_async_copy(ab_hbm, ablk.at[:, pl.ds(0, SLOTS)], local_sems.at[1])
    load_b = pltpu.make_async_copy(bb_hbm, bblk.at[:, pl.ds(0, SLOTS)], local_sems.at[2])
    load_d = pltpu.make_async_copy(diag_hbm, diag, local_sems.at[3])

    barrier = pltpu.get_barrier_semaphore()
    for link in target:
        pl.semaphore_signal(barrier, inc=1, device_id=target[link], device_id_type=MESH)
    load_b.start()
    load_a.start()
    load_d.start()
    pl.semaphore_wait(barrier, len(target))

    xi = {}
    zp = {}
    zm = {}
    sib = {}
    load_own.wait()
    for p in ("n0", "n1", "f0", "f1"):
        q = {"n0": "f0", "n1": "f1", "f0": "n0", "f1": "n1"}[p]
        xi[p] = send("xi", rows(own, p), rows(gathered[1, 0, 0], p))
        zp[q] = send("z+", rows(own, q), rows(gathered[0, 1, 0], q))
        zm[q] = send("z-", rows(own, q), rows(gathered[0, 3, 0], q))
    sib[0, 0] = [send("s", own, gathered[0, 0, 1])]

    def to_sibling(dx, dz, p):
        sib.setdefault((dx, dz), []).append(
            send("s", rows(gathered[dx, dz, 0], p), rows(gathered[dx, dz, 1], p))
        )

    def by_column(src, dst):
        def group(t, carry):
            for j in range(RB):
                dst[j, pl.ds(pl.multiple_of(t * 16, 16), 16), :] = src[t, :, j * BLK : (j + 1) * BLK]
            return carry

        lax.fori_loop(0, GROUPS, group, 0)

    def stage(q, src):
        for dy in (2, 1, 3):
            for s in range(CAP_B):
                at = sel_b[(beta_at(0, dy) % 4) * 8 + q * 4 + s]
                staged[q, dy][s] = src[at]

    sent_b = {}

    def send_staged(q):
        for up, link in enumerate(("y-", "y+")):
            half = staged[q, 2].at[pl.ds(up * 2, 2)]
            sent_b[q, "far", up] = send(link, half, relay[q, up])
        sent_b[q, 1] = send("y+", staged[q, 1], message[q, 1])
        sent_b[q, 3] = send("y-", staged[q, 3], message[q, 3])

    def pass_on(q):
        for up, link in enumerate(("y-", "y+")):
            sent_b[q, "far", up].wait_recv()
            sent_b[q, 2, up] = send(link, relay[q, up], message[q, 2].at[pl.ds(up * 2, 2)])

    def arrived_b(q, dy):
        if dy == 2:
            sent_b[q, 2, 0].wait_recv()
            sent_b[q, 2, 1].wait_recv()
        else:
            sent_b[q, dy].wait_recv()

    def alpha_chip(dx, dz):
        if not COMPUTE:
            return
        sources = [own if (dx, dz) == (0, 0) else gathered[dx, dz, 0], gathered[dx, dz, 1]]
        for dc in range(2):
            owner = alpha_at(dx, 4 - dz, dc)
            for s in range(CAP_A):
                for r in range(RA):
                    k = inv_a[r * 32 + owner * 2 + s]
                    wa[r * BLK : (r + 1) * BLK, (dc * 2 + s) * BLK : (dc * 2 + s + 1) * BLK] = ablk[r, k]
                pick = sel_a[owner * 2 + s] * PER
                for t in range(PER):
                    at = (dc * 2 + s) * BLK + t * 16
                    xa[at : at + 16, :] = sources[dc][pick + t]

        def tile(n, carry):
            cols = pl.ds(pl.multiple_of(n * 256, 256), 256)
            acc[:, cols] += jnp.dot(wa[...], xa[:, cols], preferred_element_type=jnp.float32)
            return carry

        lax.fori_loop(0, COLS // 256, tile, 0)

    def beta_owner(dxh, dy, load):
        if not COMPUTE:
            return
        owner = beta_at(dxh, 4 - dy)
        for s in range(CAP_B):
            for r in range(RB):
                k = inv_b[r * 32 + owner * 4 + s]
                wb[r * BLK : (r + 1) * BLK, s * BLK : (s + 1) * BLK] = bblk[r, k]
            load(s)

        def tile(n, carry):
            cols = pl.ds(pl.multiple_of(n * 256, 256), 256)
            acc[:, cols] += lax.dot_general(
                xb[...], wb[cols, :], (((1,), (1,)), ((), ())), preferred_element_type=jnp.float32
            )
            return carry

        lax.fori_loop(0, COLS // 256, tile, 0)

    def beta_local(q, src):
        def load(s):
            at = sel_b[y * 8 + q * 4 + s]
            xb[:, s * BLK : (s + 1) * BLK] = src[at]

        beta_owner(q, 0, load)

    def beta_message(q, dy):
        arrived_b(q, dy)

        def load(s):
            xb[:, s * BLK : (s + 1) * BLK] = message[q, dy][s]

        beta_owner(q, dy, load)

    by_column(own, own_cb)
    stage(0, own_cb)
    load_d.wait()

    def init(n, carry):
        at = pl.ds(pl.multiple_of(n * 64, 64), 64)
        acc[at, :] = diag[at, :] * own[pl.ds(n * 4, 4)].astype(jnp.float32).reshape(64, COLS)
        return carry

    lax.fori_loop(0, ROWS // 64, init, 0)
    for r in range(RA):
        ablk[r, SLOTS] = jnp.zeros((BLK, BLK), jnp.bfloat16)
    for r in range(RB):
        bblk[r, SLOTS] = jnp.zeros((BLK, BLK), jnp.bfloat16)
    send_staged(0)
    load_a.wait()
    load_b.wait()
    xf = {}
    xo = {}

    def z_first(p):
        zp[p].wait_recv()
        zm[p].wait_recv()
        for dz in (1, 3):
            xf[dz, p] = send("xi", rows(gathered[0, dz, 0], p), rows(gathered[1, dz, 0], p))
            to_sibling(0, dz, p)

    far = {}

    def forward(dx, p):
        if p in ("f0", "n0"):
            far[dx, p] = send("z+", rows(gathered[dx, 1, 0], p), rows(gathered[dx, 2, 0], p))
        else:
            far[dx, p] = send("z-", rows(gathered[dx, 3, 0], p), rows(gathered[dx, 2, 0], p))

    znp, znm = {}, {}

    def x_first(p, along_z):
        xi[p].wait_recv()
        xo[p] = send("xo", rows(gathered[1, 0, 0], p), rows(peer, p))
        if along_z:
            znp[p] = send("z+", rows(gathered[1, 0, 0], p), rows(gathered[1, 1, 0], p))
            znm[p] = send("z-", rows(gathered[1, 0, 0], p), rows(gathered[1, 3, 0], p))
        to_sibling(1, 0, p)

    z_first("f0")
    forward(0, "f0")
    x_first("n0", True)
    beta_local(0, own_cb)
    z_first("f1")
    forward(0, "f1")
    pass_on(0)
    x_first("n1", True)
    sib[0, 0][0].wait_recv()
    alpha_chip(0, 0)
    zp["n0"].wait_recv()
    zm["n0"].wait_recv()
    forward(0, "n0")
    to_sibling(0, 1, "n0")
    to_sibling(0, 3, "n0")
    x_first("f0", False)
    beta_message(0, 1)
    zp["n1"].wait_recv()
    zm["n1"].wait_recv()
    forward(0, "n1")
    to_sibling(0, 1, "n1")
    to_sibling(0, 3, "n1")
    x_first("f1", False)
    beta_message(0, 3)
    for p in ("f0", "f1"):
        far[0, p].wait_recv()
        xf[2, p] = send("xi", rows(gathered[0, 2, 0], p), rows(gathered[1, 2, 0], p))
        to_sibling(0, 2, p)
    for p in PIECES:
        xo[p].wait_recv()
    by_column(peer, peer_cb)
    stage(1, peer_cb)
    for s in sib[0, 1]:
        s.wait_recv()
    alpha_chip(0, 1)
    send_staged(1)
    for p in ("n0", "n1"):
        znp[p].wait_recv()
        znm[p].wait_recv()
        forward(1, p)
        to_sibling(1, 1, p)
        to_sibling(1, 3, p)
    for s in sib[0, 3]:
        s.wait_recv()
    alpha_chip(0, 3)
    beta_local(1, peer_cb)
    pass_on(1)
    beta_message(0, 2)
    for s in sib[1, 0]:
        s.wait_recv()
    alpha_chip(1, 0)
    for dz in (1, 3):
        for p in ("f0", "f1"):
            xf[dz, p].wait_recv()
            to_sibling(1, dz, p)
    beta_message(1, 1)
    beta_message(1, 3)
    for s in sib[1, 1]:
        s.wait_recv()
    alpha_chip(1, 1)
    for p in ("n0", "n1"):
        far[0, p].wait_recv()
        to_sibling(0, 2, p)
    for s in sib[1, 3]:
        s.wait_recv()
    alpha_chip(1, 3)
    for s in sib[0, 2]:
        s.wait_recv()
    alpha_chip(0, 2)
    beta_message(1, 2)
    for p in ("f0", "f1"):
        xf[2, p].wait_recv()
        to_sibling(1, 2, p)
    for p in ("n0", "n1"):
        far[1, p].wait_recv()
        to_sibling(1, 2, p)
    for s in sib[1, 2]:
        s.wait_recv()
    alpha_chip(1, 2)

    def finish(n, carry):
        at = pl.ds(pl.multiple_of(n * 64, 64), 64)
        out_ref[at, :] = acc[at, :].astype(jnp.bfloat16)
        return carry

    lax.fori_loop(0, ROWS // 64, finish, 0)
    for copy in started:
        copy.wait_send()
    assert count[0] <= NSEM


NSEM = 128


def picks_of(lists, owners, per_owner, cap):
    ids = owners[..., None] * per_owner + jnp.arange(per_owner, dtype=jnp.int32)
    flat = lists.reshape(lists.shape[:-2] + (-1,))
    needed = jnp.any(flat[..., None, None, :] == ids[..., None], axis=-1)
    before = jnp.arange(per_owner)[:, None] > jnp.arange(per_owner)[None, :]
    rank = jnp.sum(needed[..., None, :] & before, axis=-1)
    hit = needed[..., None, :] & (rank[..., None, :] == jnp.arange(cap)[:, None])
    position = jnp.arange(per_owner, dtype=jnp.int32)
    pick = jnp.max(jnp.where(hit, position, -1), axis=-1)
    return pick


def slots_of(lists, owners, picks, per_owner):
    wanted = jnp.where(picks >= 0, owners[:, None] * per_owner + picks, -1)
    same = lists[:, None, None, :] == wanted[None, :, :, None]
    return jnp.min(jnp.where(same, jnp.arange(SLOTS, dtype=jnp.int32), SLOTS), axis=-1)


def per_device(coefficients, diagonal, alpha_blocks, alpha_lists, beta_blocks, beta_lists):
    ia, ib = lax.axis_index("alpha"), lax.axis_index("beta")
    mine_a = lax.dynamic_slice_in_dim(alpha_lists, ia * RA, RA, 0)
    mine_b = lax.dynamic_slice_in_dim(beta_lists, ib * RB, RB, 0)
    owners_a = jnp.arange(16, dtype=jnp.int32)
    owners_b = jnp.arange(8, dtype=jnp.int32)
    pick_a = picks_of(mine_a, owners_a, RA, CAP_A)
    inv_a = slots_of(mine_a, owners_a, pick_a, RA)
    pick_b = picks_of(mine_b, owners_b, RB, CAP_B)
    inv_b = slots_of(mine_b, owners_b, pick_b, RB)
    column = lax.dynamic_slice_in_dim(beta_lists, (ib // 4) * 4 * RB, 4 * RB, 0).reshape(4, 1, RB, SLOTS)
    two = jnp.stack([ib, (ib + 4) % 8]).astype(jnp.int32)[None, :, None]
    send_b = picks_of(column, two, RB, CAP_B)
    sel_a = jnp.maximum(pick_a, 0).reshape(-1)
    sel_b = jnp.maximum(send_b, 0).reshape(-1)
    scratch = [pltpu.VMEM((GROUPS, 16, COLS), jnp.bfloat16)]
    scratch += [pltpu.VMEM((RB, ROWS, BLK), jnp.bfloat16) for _ in range(2)]
    scratch += [pltpu.VMEM((GROUPS, 16, COLS), jnp.bfloat16) for _ in range(16)]
    scratch += [pltpu.VMEM((CAP_B, ROWS, BLK), jnp.bfloat16) for _ in range(6)]
    scratch += [pltpu.VMEM((2, ROWS, BLK), jnp.bfloat16) for _ in range(4)]
    scratch += [pltpu.VMEM((CAP_B, ROWS, BLK), jnp.bfloat16) for _ in range(6)]
    scratch += [
        pltpu.VMEM((RA, SLOTS + 1, BLK, BLK), jnp.bfloat16),
        pltpu.VMEM((RB, SLOTS + 1, BLK, BLK), jnp.bfloat16),
        pltpu.VMEM((ROWS, COLS), jnp.float32),
        pltpu.VMEM((ROWS, COLS), jnp.float32),
        pltpu.VMEM((ROWS, 4 * BLK), jnp.bfloat16),
        pltpu.VMEM((COLS, 4 * BLK), jnp.bfloat16),
        pltpu.VMEM((4 * BLK, COLS), jnp.bfloat16),
        pltpu.VMEM((ROWS, 4 * BLK), jnp.bfloat16),
        pltpu.SemaphoreType.DMA((NSEM,)),
        pltpu.SemaphoreType.DMA((NSEM,)),
        pltpu.SemaphoreType.DMA((4,)),
    ]
    return pl.pallas_call(
        body,
        out_shape=jax.ShapeDtypeStruct((ROWS, COLS), jnp.bfloat16),
        in_specs=[pl.BlockSpec(memory_space=pltpu.SMEM)] * 4 + [pl.BlockSpec(memory_space=pl.ANY)] * 4,
        out_specs=pl.BlockSpec(memory_space=pltpu.VMEM),
        scratch_shapes=scratch,
        compiler_params=pltpu.CompilerParams(
            collective_id=0, has_side_effects=True, vmem_limit_bytes=60 * 1024 * 1024
        ),
    )(sel_a, inv_a.reshape(-1), sel_b, inv_b.reshape(-1), coefficients.reshape(GROUPS, 16, COLS), diagonal, alpha_blocks, beta_blocks)


def solution(mesh):
    in_specs = (
        P("alpha", "beta"),
        P("alpha", "beta"),
        P("alpha", None, None, None),
        P(),
        P("beta", None, None, None),
        P(),
    )
    return jax.shard_map(
        per_device, mesh=mesh, in_specs=in_specs, out_specs=P("alpha", "beta"), check_vma=False
    )
```

time: 181 us -> 91.3 us (0.50)
  waiting for transfers between devices: 96.2 us -> 0 us
  Pallas kernels: 0 us -> 81.6 us
  matrix products: 42.8 us -> 0 us
  local copies, waits for them, and re-layouts: 20.3 us -> 6.64 us
  between operations: 13.5 us -> 0.08 us
  starting transfers between devices: 7.47 us -> 0 us
  other arithmetic: 0.79 us -> 2.8 us
    all_to_all x1 -> x0, waiting for transfers between devices: 85.8 us -> none  [per_device(): lax.all_to_all(outgoing_b, 'beta', split_axis=0, concat_axis=0, tiled=True)]
    pallas_call x0 -> x1, Pallas kernels: none -> 81.6 us  [per_device(): pl.pallas_call(body, out_shape=jax.ShapeDtypeStruct((ROWS, COLS), jnp.bfl...]
    dot_general x4 -> x0, matrix products: 42.8 us -> none  [the longest x1 25.2 us: per_device(): jnp.einsum('rjab,jbn->ran', combined, piece_blocks, preferred_element_typ...]
    gather x3 -> x0, local copies, waits for them, and re-layouts: 11.4 us -> none  [the longest x1 10.1 us: per_device(): jnp.take(arrived_b.reshape(owners_b * CAP_B, height, block), slot_ids_b,...]
    all_gather x1 -> x0, waiting for transfers between devices: 9.67 us -> none  [per_device(): piece_rows = lax.all_gather(coefficients, 'alpha', axis=0, tiled=True)]
    all_to_all x1 -> x0, starting transfers between devices: 7.47 us -> none  [per_device(): lax.all_to_all(outgoing_b, 'beta', split_axis=0, concat_axis=0, tiled=True)]
    convert_element_type x2 -> x0, local copies, waits for them, and re-layouts: 3 us -> none  [the longest x1 2.92 us: per_device(): outgoing_b = jnp.einsum('djc,mjb->dcmb', onehot_b, coefficients.reshape(h...]
  transfers between devices with their start and end apart: 2 -> 0, of which waited for: 2 -> 0; matrix products, arithmetic and copies ran while one was open for 21% -> 0% of each run, Pallas kernels for 0% -> 0%
where the time goes in v1:
time: 91.3 us; the launch traced here: 91.1 us
  Pallas kernels  81.6 us (89%)
  local copies, waits for them, and re-layouts  6.64 us (7%)
  other arithmetic  2.8 us (3%)
    pallas_call x1, Pallas kernels, per_device(): pl.pallas_call(body, out_shape=jax.ShapeDtypeStruct((ROWS, COLS), jnp.bfl...  81.6 us
    unnamed x3, local copies, waits for them, and re-layouts  2.27 us

profile of v1, /device:TPU:1, one launch (start us, length us, event | category | flops | bytes accessed | tf_op | source)
XLA Modules:
  0.0 91.1 jit_solution(15934090911701951465)
XLA Ops:
  0.0 0.0 copy-start
  0.0 0.1 add_multiply_fusion
  0.1 0.1 iota_add_fusion.2
  0.2 0.1 iota_add_fusion
  0.3 0.8 constant_dynamic-slice_fusion.2
  1.0 0.1 copy.16
  1.1 0.1 eq.128
  1.2 0.2 compare_reduce_fusion.2
  1.4 0.1 convert_reduce_fusion.2
  1.6 0.1 select_reduce_fusion.1
  1.7 0.0 copy-done
  1.7 0.1 constant_dynamic-slice_fusion
  1.7 0.1 copy.20
  1.8 0.1 eq.146
  1.9 0.3 compare_reduce_fusion
  2.2 0.2 convert_reduce_fusion
  2.4 0.1 select_reduce_fusion.2
  2.6 0.1 constant_dynamic-slice_fusion.1
  2.7 0.1 copy.19
  2.8 0.1 eq.138
  2.8 0.3 compare_reduce_fusion.1
  3.1 0.2 convert_reduce_fusion.1
  3.4 0.2 select_reduce_fusion.3
  3.6 0.6 max.20.sel_b
  4.2 0.1 copy.17
  4.3 0.7 max.18.sel_a
  5.0 0.7 select_reduce_fusion
  5.7 0.1 copy.22
  5.8 0.7 reshape.251.inv_b
  6.5 0.1 copy.18
  6.6 0.7 reshape.250.inv_a
  7.3 81.6 %shard_map.64 = bf16[512,1024]{1,0:T(8,128)(2,1)} custom-call(s32[32]{0:T(128)} %max.18.sel_a, s32[128]{0:T(128)} %reshape.250.inv_a, s32[32]{0:T(128)} %max.20.sel_b, s32[256]{0:T(256)} %reshape.251.inv_b, bf16[32,16,1024]{2,1,0:T(8,128)(2,1)} %bitcast.3, f32[512,1024]{1,0:T(8,128)} %diag_hbm.1, bf16[4,14,128,128]{3,2,1,0:T(8,128)(2,1)} %ab_hbm.1, ...), custom_call_target="tpu_custom_call" | custom-call | tf_op jit(solution)/shard_map/pallas_call | solution.py:395
  88.8 2.3 %copy.24 = bf16[512,1024]{1,0:T(8,128)(2,1)} copy(bf16[512,1024]{1,0:T(8,128)(2,1)} %shard_map.64) | data formatting | bytes 2097152
  (9 shorter events, 0.1 us)
Async XLA Ops:
  0.0 1.7 %copy-start = (s32[64,14]{0,1:T(8,128)S(1)}, s32[64,14]{0,1:T(8,128)}, u32[]{:S(2)}) copy-start(s32[64,14]{0,1:T(8,128)} %param.11) | copy-start | bytes 10756

commit v2 on v0

v2 whole, which is shorter than its diff:
```python
import jax
import jax.numpy as jnp
from jax import lax
from jax.experimental import pallas as pl
from jax.experimental.pallas import tpu as pltpu
from jax.sharding import PartitionSpec as P

MESH = pl.DeviceIdType.MESH
BLK = 128
SLOTS = 14
RA = 4
RB = 8
CAP_A = 2
CAP_B = 4
ROWS = RA * BLK
COLS = RB * BLK
GROUPS = ROWS // 16
PER = BLK // 16

PIECES = {"n0": (0, 9), "n1": (9, 9), "f0": (18, 7), "f1": (25, 7)}
N_PIECES = ("n0", "n1")
PARTS = ((0, 18), (18, 14))
F_PIECES = ("f0", "f1")
NSEM = 96
COMPUTE = True

INV_A = 0
INV_B = 8
SEL_A = 40
SEL_B = 56
TABLE = 88


def body(la_hbm, lb_hbm, c_hbm, diag_hbm, ab_hbm, bb_hbm, out_hbm, *scratch):
    it = iter(scratch)
    own, own_cb = next(it), next(it)
    gathered = {}
    for dx in range(2):
        for dz in range(4):
            for dc in range(2):
                if (dx, dz, dc) != (0, 0, 0):
                    gathered[dx, dz, dc] = next(it)
    peer = [next(it), next(it)]
    peer_cb = [next(it), next(it)]
    message = {(q, dy): next(it) for q in range(2) for dy in (1, 2, 3)}
    staged = {(q, dy): next(it) for q in range(2) for dy in (1, 2, 3)}
    la, lb, lists_a, lists_b, table, tab, ablk, bblk, diag, acc, out, wa, wb, xa, xb = (next(it) for _ in range(15))
    send_sems, recv_sems, local_sems = it

    ia, ib = lax.axis_index("alpha"), lax.axis_index("beta")
    x_lo, z, core = ia // 8, (ia // 2) % 4, ia % 2
    x_hi, y = ib // 4, ib % 4

    def alpha_at(dx, dz, dc):
        return ((x_lo + dx) % 2) * 8 + ((z + dz) % 4) * 2 + (core + dc) % 2

    def beta_at(dxh, dy):
        return ((x_hi + dxh) % 2) * 4 + (y + dy) % 4

    target = {
        "s": (alpha_at(0, 0, 1), ib),
        "xi": (alpha_at(1, 0, 0), ib),
        "xo": (alpha_at(1, 0, 0), beta_at(1, 0)),
        "z1": (alpha_at(0, 1, 0), ib),
        "z3": (alpha_at(0, 3, 0), ib),
        "y1": (ia, beta_at(0, 1)),
        "y3": (ia, beta_at(0, 3)),
        "y2": (ia, beta_at(0, 2)),
    }
    started = []

    def send(link, src, dst):
        n = len(started)
        copy = pltpu.make_async_remote_copy(
            src_ref=src,
            dst_ref=dst,
            send_sem=send_sems.at[n],
            recv_sem=recv_sems.at[n],
            device_id=target[link],
            device_id_type=MESH,
        )
        copy.start()
        started.append(copy)
        return copy

    def part(ref, piece):
        first, size = PIECES[piece]
        return ref.at[pl.ds(first, size)]

    def local(n, src, dst):
        copy = pltpu.make_async_copy(src, dst, local_sems.at[n])
        copy.start()
        return copy

    load_la = local(0, la_hbm, la)
    load_lb = local(1, lb_hbm, lb)
    load_own = local(2, c_hbm, own)
    barrier = pltpu.get_barrier_semaphore()
    for link in target:
        pl.semaphore_signal(barrier, inc=1, device_id=target[link], device_id_type=MESH)
    load_b = local(3, bb_hbm, bblk.at[:, pl.ds(0, SLOTS)])
    load_d = local(4, diag_hbm, diag)
    load_a = local(5, ab_hbm, ablk.at[:, pl.ds(0, SLOTS)])
    pl.semaphore_wait(barrier, len(target))

    xi, zn, zf, zs, sib = {}, {}, {}, {}, {}
    for p in PIECES:
        xi[p] = send("xi", part(c_hbm, p), part(gathered[1, 0, 0], p))
    zo = {}
    for p in F_PIECES:
        for dz in (1, 3):
            zo[dz, p] = send(f"z{dz}", part(c_hbm, p), part(gathered[0, dz, 0], p))
    for p in N_PIECES:
        for dz in (1, 3):
            zo[dz, p] = send(f"z{dz}", part(c_hbm, p), part(gathered[0, dz, 0], p))
    sib[0, 0] = [send("s", c_hbm, gathered[0, 0, 1])]

    def to_sibling(dx, dz, p):
        copy = send("s", part(gathered[dx, dz, 0], p), part(gathered[dx, dz, 1], p))
        sib.setdefault((dx, dz), []).append(copy)

    lane = lax.broadcasted_iota(jnp.int32, (8, BLK), 1)

    def slots_of(lists):
        inv = jnp.full((8, BLK), SLOTS, jnp.int32)
        for k in range(SLOTS):
            inv = jnp.where(lists[:, k : k + 1] == lane, k, inv)
        return inv

    def picks_of(needed, per, cap, first_row):
        place = lane % per
        shifts = [1 << i for i in range(per.bit_length() - 1)]
        rank = needed
        for shift in shifts:
            rank = rank + jnp.where(place >= shift, pltpu.roll(rank, shift, 1), 0)
        rank = rank - needed
        for s in range(cap):
            pick = jnp.where((needed > 0) & (rank == s), lane, BLK - 1)
            for shift in shifts:
                moved = pltpu.roll(pick, BLK - shift, 1)
                pick = jnp.minimum(pick, jnp.where(place + shift < per, moved, BLK - 1))
            table[first_row + 8 * s : first_row + 8 * s + 8, :] = pick

    load_la.wait()
    load_lb.wait()
    lists_a[...] = la[...].T
    lists_b[...] = lb[...].T
    inv = slots_of(lists_a[pl.ds(pl.multiple_of((ia // 2) * 8, 8), 8), :])
    table[INV_A : INV_A + 8, :] = inv
    row = lax.broadcasted_iota(jnp.int32, (8, BLK), 0)
    mine = (row // RA == core) & (inv < SLOTS)
    needed = jnp.broadcast_to(jnp.max(jnp.where(mine, 1, 0), axis=0, keepdims=True), (8, BLK))
    picks_of(needed, RA, CAP_A, SEL_A)
    needed = jnp.zeros((8, BLK), jnp.int32)
    for d in range(4):
        inv = slots_of(lists_b[pl.ds(pl.multiple_of(x_hi * 32 + d * 8, 8), 8), :])
        table[INV_B + 8 * d : INV_B + 8 * d + 8, :] = inv
        used = jnp.max(jnp.where(inv < SLOTS, 1, 0), axis=0, keepdims=True)
        needed = jnp.where(row == d, used, needed)
    picks_of(needed, RB, CAP_B, SEL_B)

    def by_column(src, dst, groups):
        def group(t, carry):
            for j in range(RB):
                dst[j, pl.ds(pl.multiple_of(t * 16, 16), 16), :] = src[t, :, j * BLK : (j + 1) * BLK]
            return carry

        lax.fori_loop(0, groups, group, 0)

    load_own.wait()
    by_column(own, own_cb, GROUPS)
    for r in range(RA):
        ablk[r, SLOTS] = jnp.zeros((BLK, BLK), jnp.bfloat16)
    for r in range(RB):
        bblk[r, SLOTS] = jnp.zeros((BLK, BLK), jnp.bfloat16)
    load_tab = local(6, table, tab)
    load_tab.wait()

    def pick_b(d, q, s):
        return tab[SEL_B + 8 * s + (y + d) % 4, beta_at(q, 0) * RB] % RB

    sent_b = {}

    def stage_own():
        for dy in (2, 1, 3):
            for s in range(CAP_B):
                staged[0, dy][s] = own_cb[pick_b(dy, 0, s)]

    def send_own():
        for dy in (2, 1, 3):
            sent_b[0, dy] = [send(f"y{dy}", staged[0, dy], message[0, dy])]

    def stage_peer(h):
        for dy in (2, 1, 3):
            for s in range(CAP_B):
                staged[1, dy][s, pl.ds(PARTS[h][0] * 16, PARTS[h][1] * 16), :] = peer_cb[h][pick_b(dy, 1, s)]

    def send_peer(h):
        for dy in (2, 1, 3):
            at = (slice(None), pl.ds(PARTS[h][0] * 16, PARTS[h][1] * 16))
            copy = send(f"y{dy}", staged[1, dy].at[at], message[1, dy].at[at])
            sent_b.setdefault((1, dy), []).append(copy)

    def alpha_weights(dx, dz):
        for dc in range(2):
            owner = alpha_at(dx, 4 - dz, dc)
            for s in range(CAP_A):
                column = (dc * CAP_A + s) * BLK
                pick = tab[SEL_A + 8 * s, owner * RA]
                for r in range(RA):
                    wa[r * BLK : (r + 1) * BLK, column : column + BLK] = ablk[r, tab[INV_A + core * RA + r, pick]]

    def alpha_inputs(dx, dz):
        for dc in range(2):
            owner = alpha_at(dx, 4 - dz, dc)
            source = own if (dx, dz, dc) == (0, 0, 0) else gathered[dx, dz, dc]
            for s in range(CAP_A):
                first = (tab[SEL_A + 8 * s, owner * RA] % RA) * PER
                for t in range(PER):
                    at = (dc * CAP_A + s) * BLK + t * 16
                    xa[at : at + 16, :] = source[first + t]

    def tiles(one):
        def tile(n, carry):
            one(pl.ds(pl.multiple_of(n * 256, 256), 256))
            return carry

        lax.fori_loop(0, COLS // 256, tile, 0)

    def alpha_dot(cols):
        return jnp.dot(wa[...], xa[:, cols], preferred_element_type=jnp.float32)

    def add_alpha(cols):
        acc[:, cols] += alpha_dot(cols)

    def add_beta(cols):
        acc[:, cols] += lax.dot_general(
            xb[...], wb[cols, :], (((1,), (1,)), ((), ())), preferred_element_type=jnp.float32
        )

    def alpha_chip(dx, dz):
        if not COMPUTE:
            return
        alpha_weights(dx, dz)
        alpha_inputs(dx, dz)
        tiles(add_alpha)

    def beta_owner(q, dy):
        if not COMPUTE:
            return
        owner = beta_at(q, 4 - dy)
        for s in range(CAP_B):
            pick = tab[SEL_B + 8 * s + y, owner * RB]
            for r in range(RB):
                wb[r * BLK : (r + 1) * BLK, s * BLK : (s + 1) * BLK] = bblk[r, tab[INV_B + y * RB + r, pick]]
            column = slice(s * BLK, (s + 1) * BLK)
            if dy:
                xb[:, column] = message[q, dy][s]
            elif q:
                for h in range(2):
                    xb[pl.ds(PARTS[h][0] * 16, PARTS[h][1] * 16), column] = peer_cb[h][pick % RB]
            else:
                xb[:, column] = own_cb[pick % RB]
        tiles(add_beta)

    def arrived(copies):
        for copy in copies:
            copy.wait_recv()

    stage_own()
    load_d.wait()

    def init(n, carry):
        at = pl.ds(pl.multiple_of(n * 64, 64), 64)
        acc[at, :] = diag[at, :] * own[pl.ds(n * 4, 4)].astype(jnp.float32).reshape(64, COLS)
        return carry

    lax.fori_loop(0, ROWS // 64, init, 0)
    send_own()
    load_b.wait()
    load_a.wait()
    beta_owner(0, 0)
    arrived(sib[0, 0])
    alpha_chip(0, 0)

    xo = {}

    def over_x(p):
        h = 0 if p in N_PIECES else 1
        first, size = PIECES[p]
        xi[p].wait_recv()
        xo[p] = send("xo", part(gathered[1, 0, 0], p), peer[h].at[pl.ds(first - PARTS[h][0], size)])
        to_sibling(1, 0, p)

    def from_z(copies, dx, dz, pieces):
        for p in pieces:
            copies[dz, p].wait_recv()
            to_sibling(dx, dz, p)

    zx = {}

    def relay(copies, dx, p):
        dz = 1 if p in ("n0", "f0") else 3
        copies[2, p] = send(f"z{dz}", part(gathered[dx, dz, 0], p), part(gathered[dx, 2, 0], p))

    def near_z(copies, dx, p):
        copies[1, p].wait_recv()
        copies[3, p].wait_recv()
        relay(copies, dx, p)
        to_sibling(dx, 1, p)
        to_sibling(dx, 3, p)

    def x_after_z(dz, pieces):
        for p in pieces:
            zx[dz, p] = send("xi", part(gathered[0, dz, 0], p), part(gathered[1, dz, 0], p))

    near_z(zo, 0, "f0")
    over_x("n0")
    near_z(zo, 0, "f1")
    x_after_z(1, F_PIECES)
    x_after_z(3, F_PIECES)
    over_x("n1")
    for p in N_PIECES:
        for dz in (1, 3):
            zx[dz, p] = send(f"z{dz}", part(gathered[1, 0, 0], p), part(gathered[1, dz, 0], p))
    arrived(sent_b[0, 2])
    beta_owner(0, 2)
    near_z(zo, 0, "n0")
    over_x("f0")
    arrived([xo["n0"], xo["n1"]])
    by_column(peer[0], peer_cb[0], PARTS[0][1])
    stage_peer(0)
    near_z(zo, 0, "n1")
    over_x("f1")
    send_peer(0)
    arrived(sent_b[0, 1])
    beta_owner(0, 1)
    arrived(sent_b[0, 3])
    beta_owner(0, 3)
    from_z(zo, 0, 2, F_PIECES)
    x_after_z(2, F_PIECES)
    arrived([xo["f0"], xo["f1"]])
    by_column(peer[1], peer_cb[1], PARTS[1][1])
    stage_peer(1)
    arrived(sib[1, 0])
    alpha_chip(1, 0)
    send_peer(1)
    near_z(zx, 1, "n0")
    arrived(sib[0, 1])
    alpha_chip(0, 1)
    beta_owner(1, 0)
    arrived(sib[0, 3])
    alpha_chip(0, 3)
    near_z(zx, 1, "n1")
    from_z(zx, 1, 1, F_PIECES)
    arrived(sib[1, 1])
    alpha_chip(1, 1)
    arrived(sent_b[1, 2])
    beta_owner(1, 2)
    from_z(zx, 1, 3, F_PIECES)
    arrived(sib[1, 3])
    alpha_chip(1, 3)
    arrived(sent_b[1, 1])
    beta_owner(1, 1)
    arrived(sent_b[1, 3])
    beta_owner(1, 3)
    from_z(zo, 0, 2, N_PIECES)
    arrived(sib[0, 2])
    alpha_chip(0, 2)
    alpha_weights(1, 2)
    from_z(zx, 1, 2, F_PIECES)
    from_z(zx, 1, 2, N_PIECES)
    arrived(sib[1, 2])
    alpha_inputs(1, 2)

    def last(n, carry):
        cols = pl.ds(pl.multiple_of(n * 256, 256), 256)
        out[:, cols] = (acc[:, cols] + alpha_dot(cols)).astype(jnp.bfloat16)
        return carry

    lax.fori_loop(0, COLS // 256, last, 0)
    store = local(7, out, out_hbm)
    for copy in started:
        copy.wait_send()
    store.wait()
    assert len(started) <= NSEM, len(started)


def per_device(coefficients, diagonal, alpha_blocks, alpha_lists, beta_blocks, beta_lists):
    grouped = pltpu.VMEM((GROUPS, 16, COLS), jnp.bfloat16)
    by_block = pltpu.VMEM((RB, ROWS, BLK), jnp.bfloat16)
    slots = pltpu.VMEM((CAP_B, ROWS, BLK), jnp.bfloat16)
    scratch = [grouped, by_block] + [grouped] * 15 + [pltpu.VMEM((n, 16, COLS), jnp.bfloat16) for _, n in PARTS]
    scratch += [pltpu.VMEM((RB, n * 16, BLK), jnp.bfloat16) for _, n in PARTS] + [slots] * 12
    scratch += [
        pltpu.VMEM((SLOTS, 64), jnp.int32),
        pltpu.VMEM((SLOTS, 64), jnp.int32),
        pltpu.VMEM((64, SLOTS), jnp.int32),
        pltpu.VMEM((64, SLOTS), jnp.int32),
        pltpu.VMEM((TABLE, BLK), jnp.int32),
        pltpu.SMEM((TABLE, BLK), jnp.int32),
        pltpu.VMEM((RA, SLOTS + 1, BLK, BLK), jnp.bfloat16),
        pltpu.VMEM((RB, SLOTS + 1, BLK, BLK), jnp.bfloat16),
        pltpu.VMEM((ROWS, COLS), jnp.float32),
        pltpu.VMEM((ROWS, COLS), jnp.float32),
        pltpu.VMEM((ROWS, COLS), jnp.bfloat16),
        pltpu.VMEM((ROWS, 4 * BLK), jnp.bfloat16),
        pltpu.VMEM((COLS, 4 * BLK), jnp.bfloat16),
        pltpu.VMEM((4 * BLK, COLS), jnp.bfloat16),
        pltpu.VMEM((ROWS, 4 * BLK), jnp.bfloat16),
        pltpu.SemaphoreType.DMA((NSEM,)),
        pltpu.SemaphoreType.DMA((NSEM,)),
        pltpu.SemaphoreType.DMA((8,)),
    ]
    return pl.pallas_call(
        body,
        out_shape=jax.ShapeDtypeStruct((ROWS, COLS), jnp.bfloat16),
        in_specs=[pl.BlockSpec(memory_space=pl.ANY)] * 6,
        out_specs=pl.BlockSpec(memory_space=pl.ANY),
        scratch_shapes=scratch,
        compiler_params=pltpu.CompilerParams(
            collective_id=0, has_side_effects=True, vmem_limit_bytes=60 * 1024 * 1024
        ),
    )(
        alpha_lists.T,
        beta_lists.T,
        coefficients.reshape(GROUPS, 16, COLS),
        diagonal,
        alpha_blocks,
        beta_blocks,
    )


def solution(mesh):
    in_specs = (
        P("alpha", "beta"),
        P("alpha", "beta"),
        P("alpha", None, None, None),
        P(),
        P("beta", None, None, None),
        P(),
    )
    return jax.shard_map(
        per_device, mesh=mesh, in_specs=in_specs, out_specs=P("alpha", "beta"), check_vma=False
    )
```

time: 181 us -> 74.3 us (0.41)
  waiting for transfers between devices: 96.2 us -> 0 us
  Pallas kernels: 0 us -> 71.8 us
  matrix products: 42.8 us -> 0 us
  local copies, waits for them, and re-layouts: 20.3 us -> 2.26 us
  between operations: 13.5 us -> 0.01 us
  starting transfers between devices: 7.47 us -> 0 us
    all_to_all x1 -> x0, waiting for transfers between devices: 85.8 us -> none  [per_device(): lax.all_to_all(outgoing_b, 'beta', split_axis=0, concat_axis=0, tiled=True)]
    pallas_call x0 -> x1, Pallas kernels: none -> 71.8 us  [per_device(): pl.pallas_call(body, out_shape=jax.ShapeDtypeStruct((ROWS, COLS), jnp.bfl...]
    dot_general x4 -> x0, matrix products: 42.8 us -> none  [the longest x1 25.2 us: per_device(): jnp.einsum('rjab,jbn->ran', combined, piece_blocks, preferred_element_typ...]
    gather x3 -> x0, local copies, waits for them, and re-layouts: 11.4 us -> none  [the longest x1 10.1 us: per_device(): jnp.take(arrived_b.reshape(owners_b * CAP_B, height, block), slot_ids_b,...]
    all_gather x1 -> x0, waiting for transfers between devices: 9.67 us -> none  [per_device(): piece_rows = lax.all_gather(coefficients, 'alpha', axis=0, tiled=True)]
    all_to_all x1 -> x0, starting transfers between devices: 7.47 us -> none  [per_device(): lax.all_to_all(outgoing_b, 'beta', split_axis=0, concat_axis=0, tiled=True)]
    reshape x1 -> x0, local copies, waits for them, and re-layouts: 3.04 us -> none  [per_device(): beta_term = jnp.einsum('rkmb,rkab->mra', chosen_b, beta_blocks, preferred...]
    convert_element_type x2 -> x0, local copies, waits for them, and re-layouts: 3 us -> none  [the longest x1 2.92 us: per_device(): outgoing_b = jnp.einsum('djc,mjb->dcmb', onehot_b, coefficients.reshape(h...]
  transfers between devices with their start and end apart: 2 -> 0, of which waited for: 2 -> 0; matrix products, arithmetic and copies ran while one was open for 21% -> 0% of each run, Pallas kernels for 0% -> 0%
where the time goes in v2:
time: 74.3 us; the launch traced here: 74.1 us
  Pallas kernels  71.8 us (97%)
  local copies, waits for them, and re-layouts  2.26 us (3%)
    pallas_call x1, Pallas kernels, per_device(): pl.pallas_call(body, out_shape=jax.ShapeDtypeStruct((ROWS, COLS), jnp.bfl...  71.8 us
    unnamed x1, local copies, waits for them, and re-layouts  2.26 us

profile of v2, /device:TPU:1, one launch (start us, length us, event | category | flops | bytes accessed | tf_op | source)
XLA Modules:
  0.0 74.1 jit_solution(17855442242212074353)
XLA Ops:
  0.0 71.8 %shard_map.64 = bf16[512,1024]{1,0:T(8,128)(2,1)} custom-call(s32[14,64]{1,0:T(8,128)} %bitcast.4, s32[14,64]{1,0:T(8,128)} %bitcast.5, bf16[32,16,1024]{2,1,0:T(8,128)(2,1)} %bitcast.3, f32[512,1024]{1,0:T(8,128)} %diag_hbm.1, bf16[4,14,128,128]{3,2,1,0:T(8,128)(2,1)} %ab_hbm.1, bf16[8,14,128,128]{3,2,1,0:T(8,128)(2,1)} %bb_hbm.1), custom_call_target="tpu_custom_call" | custom-call | tf_op jit(solution)/shard_map/pallas_call | solution.py:415
  71.9 2.3 %copy.8 = bf16[512,1024]{1,0:T(8,128)(2,1)} copy(bf16[512,1024]{1,0:T(8,128)(2,1)} %shard_map.64) | data formatting | bytes 2097152

commit v3 on v2

--- a/solution.py
+++ b/solution.py
@@ -31,7 +31,7 @@
 TABLE = 88
 
 
-def body(la_hbm, lb_hbm, c_hbm, diag_hbm, ab_hbm, bb_hbm, out_hbm, *scratch):
+def body(la_hbm, lb_hbm, c_hbm, diag_hbm, ab_hbm, bb_hbm, out_ref, *scratch):
     it = iter(scratch)
     own, own_cb = next(it), next(it)
     gathered = {}
@@ -44,7 +44,7 @@
     peer_cb = [next(it), next(it)]
     message = {(q, dy): next(it) for q in range(2) for dy in (1, 2, 3)}
     staged = {(q, dy): next(it) for q in range(2) for dy in (1, 2, 3)}
-    la, lb, lists_a, lists_b, table, tab, ablk, bblk, diag, acc, out, wa, wb, xa, xb = (next(it) for _ in range(15))
+    la, lb, lists_a, lists_b, table, tab, ablk, bblk, diag, acc, wa, wb, xa, xb = (next(it) for _ in range(14))
     send_sems, recv_sems, local_sems = it
 
     ia, ib = lax.axis_index("alpha"), lax.axis_index("beta")
@@ -169,10 +169,6 @@
 
     load_own.wait()
     by_column(own, own_cb, GROUPS)
-    for r in range(RA):
-        ablk[r, SLOTS] = jnp.zeros((BLK, BLK), jnp.bfloat16)
-    for r in range(RB):
-        bblk[r, SLOTS] = jnp.zeros((BLK, BLK), jnp.bfloat16)
     load_tab = local(6, table, tab)
     load_tab.wait()
 
@@ -210,8 +206,8 @@
                 for r in range(RA):
                     wa[r * BLK : (r + 1) * BLK, column : column + BLK] = ablk[r, tab[INV_A + core * RA + r, pick]]
 
-    def alpha_inputs(dx, dz):
-        for dc in range(2):
+    def alpha_inputs(dx, dz, *lanes):
+        for dc in lanes:
             owner = alpha_at(dx, 4 - dz, dc)
             source = own if (dx, dz, dc) == (0, 0, 0) else gathered[dx, dz, dc]
             for s in range(CAP_A):
@@ -227,11 +223,15 @@
 
         lax.fori_loop(0, COLS // 256, tile, 0)
 
-    def alpha_dot(cols):
-        return jnp.dot(wa[...], xa[:, cols], preferred_element_type=jnp.float32)
+    def alpha_dot(cols, *lanes):
+        depth = pl.ds(lanes[0] * CAP_A * BLK, len(lanes) * CAP_A * BLK)
+        return jnp.dot(wa[:, depth], xa[depth, cols], preferred_element_type=jnp.float32)
 
     def add_alpha(cols):
-        acc[:, cols] += alpha_dot(cols)
+        acc[:, cols] += alpha_dot(cols, 0, 1)
+
+    def add_alpha_lane(cols):
+        acc[:, cols] += alpha_dot(cols, 0)
 
     def add_beta(cols):
         acc[:, cols] += lax.dot_general(
@@ -242,7 +242,7 @@
         if not COMPUTE:
             return
         alpha_weights(dx, dz)
-        alpha_inputs(dx, dz)
+        alpha_inputs(dx, dz, 0, 1)
         tiles(add_alpha)
 
     def beta_owner(q, dy):
@@ -268,6 +268,11 @@
             copy.wait_recv()
 
     stage_own()
+    for r in range(RA):
+        ablk[r, SLOTS] = jnp.zeros((BLK, BLK), jnp.bfloat16)
+    for r in range(RB):
+        bblk[r, SLOTS] = jnp.zeros((BLK, BLK), jnp.bfloat16)
+    send_own()
     load_d.wait()
 
     def init(n, carry):
@@ -276,7 +281,6 @@
         return carry
 
     lax.fori_loop(0, ROWS // 64, init, 0)
-    send_own()
     load_b.wait()
     load_a.wait()
     beta_owner(0, 0)
@@ -342,6 +346,7 @@
     arrived([xo["f0"], xo["f1"]])
     by_column(peer[1], peer_cb[1], PARTS[1][1])
     stage_peer(1)
+    from_z(zx, 1, 1, F_PIECES)
     arrived(sib[1, 0])
     alpha_chip(1, 0)
     send_peer(1)
@@ -352,37 +357,36 @@
     arrived(sib[0, 3])
     alpha_chip(0, 3)
     near_z(zx, 1, "n1")
-    from_z(zx, 1, 1, F_PIECES)
     arrived(sib[1, 1])
     alpha_chip(1, 1)
+    from_z(zx, 1, 3, F_PIECES)
     arrived(sent_b[1, 2])
     beta_owner(1, 2)
-    from_z(zx, 1, 3, F_PIECES)
     arrived(sib[1, 3])
     alpha_chip(1, 3)
+    from_z(zo, 0, 2, N_PIECES)
+    from_z(zx, 1, 2, ("f0",))
     arrived(sent_b[1, 1])
     beta_owner(1, 1)
     arrived(sent_b[1, 3])
     beta_owner(1, 3)
-    from_z(zo, 0, 2, N_PIECES)
     arrived(sib[0, 2])
     alpha_chip(0, 2)
     alpha_weights(1, 2)
-    from_z(zx, 1, 2, F_PIECES)
-    from_z(zx, 1, 2, N_PIECES)
+    from_z(zx, 1, 2, ("f1",) + N_PIECES)
+    alpha_inputs(1, 2, 0)
+    tiles(add_alpha_lane)
     arrived(sib[1, 2])
-    alpha_inputs(1, 2)
+    alpha_inputs(1, 2, 1)
 
     def last(n, carry):
         cols = pl.ds(pl.multiple_of(n * 256, 256), 256)
-        out[:, cols] = (acc[:, cols] + alpha_dot(cols)).astype(jnp.bfloat16)
+        out_ref[:, cols] = (acc[:, cols] + alpha_dot(cols, 1)).astype(jnp.bfloat16)
         return carry
 
     lax.fori_loop(0, COLS // 256, last, 0)
-    store = local(7, out, out_hbm)
     for copy in started:
         copy.wait_send()
-    store.wait()
     assert len(started) <= NSEM, len(started)
 
 
@@ -403,20 +407,19 @@
         pltpu.VMEM((RB, SLOTS + 1, BLK, BLK), jnp.bfloat16),
         pltpu.VMEM((ROWS, COLS), jnp.float32),
         pltpu.VMEM((ROWS, COLS), jnp.float32),
-        pltpu.VMEM((ROWS, COLS), jnp.bfloat16),
         pltpu.VMEM((ROWS, 4 * BLK), jnp.bfloat16),
         pltpu.VMEM((COLS, 4 * BLK), jnp.bfloat16),
         pltpu.VMEM((4 * BLK, COLS), jnp.bfloat16),
         pltpu.VMEM((ROWS, 4 * BLK), jnp.bfloat16),
         pltpu.SemaphoreType.DMA((NSEM,)),
         pltpu.SemaphoreType.DMA((NSEM,)),
-        pltpu.SemaphoreType.DMA((8,)),
+        pltpu.SemaphoreType.DMA((7,)),
     ]
     return pl.pallas_call(
         body,
-        out_shape=jax.ShapeDtypeStruct((ROWS, COLS), jnp.bfloat16),
+        out_shape=pltpu.VMEM((ROWS, COLS), jnp.bfloat16),
         in_specs=[pl.BlockSpec(memory_space=pl.ANY)] * 6,
-        out_specs=pl.BlockSpec(memory_space=pl.ANY),
+        out_specs=pl.BlockSpec(memory_space=pltpu.VMEM),
         scratch_shapes=scratch,
         compiler_params=pltpu.CompilerParams(
             collective_id=0, has_side_effects=True, vmem_limit_bytes=60 * 1024 * 1024

time: 74.3 us -> 68.1 us (0.917)
  Pallas kernels: 71.8 us -> 67 us
  local copies, waits for them, and re-layouts: 2.26 us -> 0.97 us
    pallas_call x1, Pallas kernels: 71.8 us -> 67 us  [per_device(): pl.pallas_call(body, out_shape=pltpu.VMEM((ROWS, COLS), jnp.bfloat16), in...]
    unnamed x1, local copies, waits for them, and re-layouts: 2.26 us -> 0.97 us
where the time goes in v3:
time: 68.1 us; the launch traced here: 68 us
  Pallas kernels  67 us (98%)
  local copies, waits for them, and re-layouts  0.97 us (1%)
    pallas_call x1, Pallas kernels, per_device(): pl.pallas_call(body, out_shape=pltpu.VMEM((ROWS, COLS), jnp.bfloat16), in...  67 us

profile of v3, /device:TPU:1, one launch (start us, length us, event | category | flops | bytes accessed | tf_op | source)
XLA Modules:
  0.0 68.0 jit_solution(14865864061457796018)
XLA Ops:
  0.0 67.0 %shard_map.64 = bf16[512,1024]{1,0:T(8,128)(2,1)S(1)} custom-call(s32[14,64]{1,0:T(8,128)} %bitcast.4, s32[14,64]{1,0:T(8,128)} %bitcast.5, bf16[32,16,1024]{2,1,0:T(8,128)(2,1)} %bitcast.3, f32[512,1024]{1,0:T(8,128)} %diag_hbm.1, bf16[4,14,128,128]{3,2,1,0:T(8,128)(2,1)} %ab_hbm.1, bf16[8,14,128,128]{3,2,1,0:T(8,128)(2,1)} %bb_hbm.1), custom_call_target="tpu_custom_call" | custom-call | tf_op jit(solution)/shard_map/pallas_call | solution.py:418
  67.0 1.0 %copy.8 = bf16[512,1024]{1,0:T(8,128)(2,1)} copy(bf16[512,1024]{1,0:T(8,128)(2,1)S(1)} %shard_map.64) | data formatting | bytes 2097152

commit v4 on v3

--- a/solution.py
+++ b/solution.py
@@ -17,10 +17,21 @@
 GROUPS = ROWS // 16
 PER = BLK // 16
 
-PIECES = {"n0": (0, 9), "n1": (9, 9), "f0": (18, 7), "f1": (25, 7)}
-N_PIECES = ("n0", "n1")
-PARTS = ((0, 18), (18, 14))
-F_PIECES = ("f0", "f1")
+PIECES = {
+    "n": (0, 17),
+    "n0": (0, 8),
+    "n1": (8, 9),
+    "n0a": (0, 5),
+    "n0b": (5, 3),
+    "n1a": (8, 6),
+    "n1b": (14, 3),
+    "f": (17, 15),
+    "f0": (17, 8),
+    "f1": (25, 7),
+    "fa": (17, 11),
+    "fb": (28, 4),
+}
+PARTS = (PIECES["n"], PIECES["f"])
 NSEM = 96
 COMPUTE = True
 
@@ -104,13 +115,10 @@
     pl.semaphore_wait(barrier, len(target))
 
     xi, zn, zf, zs, sib = {}, {}, {}, {}, {}
-    for p in PIECES:
+    for p in ("n0", "n1", "f0", "f1"):
         xi[p] = send("xi", part(c_hbm, p), part(gathered[1, 0, 0], p))
     zo = {}
-    for p in F_PIECES:
-        for dz in (1, 3):
-            zo[dz, p] = send(f"z{dz}", part(c_hbm, p), part(gathered[0, dz, 0], p))
-    for p in N_PIECES:
+    for p in ("f", "n"):
         for dz in (1, 3):
             zo[dz, p] = send(f"z{dz}", part(c_hbm, p), part(gathered[0, dz, 0], p))
     sib[0, 0] = [send("s", c_hbm, gathered[0, 0, 1])]
@@ -167,9 +175,13 @@
 
         lax.fori_loop(0, groups, group, 0)
 
+    for r in range(RA):
+        ablk[r, SLOTS] = jnp.zeros((BLK, BLK), jnp.bfloat16)
+    for r in range(RB):
+        bblk[r, SLOTS] = jnp.zeros((BLK, BLK), jnp.bfloat16)
     load_own.wait()
+    load_tab = local(6, table, tab)
     by_column(own, own_cb, GROUPS)
-    load_tab = local(6, table, tab)
     load_tab.wait()
 
     def pick_b(d, q, s):
@@ -268,10 +280,6 @@
             copy.wait_recv()
 
     stage_own()
-    for r in range(RA):
-        ablk[r, SLOTS] = jnp.zeros((BLK, BLK), jnp.bfloat16)
-    for r in range(RB):
-        bblk[r, SLOTS] = jnp.zeros((BLK, BLK), jnp.bfloat16)
     send_own()
     load_d.wait()
 
@@ -290,90 +298,88 @@
     xo = {}
 
     def over_x(p):
-        h = 0 if p in N_PIECES else 1
+        h = int(p in ("f0", "f1"))
         first, size = PIECES[p]
         xi[p].wait_recv()
         xo[p] = send("xo", part(gathered[1, 0, 0], p), peer[h].at[pl.ds(first - PARTS[h][0], size)])
-        to_sibling(1, 0, p)
-
-    def from_z(copies, dx, dz, pieces):
+
+    zx = {}
+
+    def relay(copies, dx, *pieces):
+        for p in pieces:
+            dz = 1 if p[:2] in ("n0", "f0") else 3
+            copies[2, p] = send(f"z{dz}", part(gathered[dx, dz, 0], p), part(gathered[dx, 2, 0], p))
+
+    def near_z(copies, dx, p, *halves):
+        for dz in (1, 3):
+            copies[dz, p].wait_recv()
+        relay(copies, dx, *halves)
+        for dz in (1, 3):
+            to_sibling(dx, dz, p)
+
+    def after(copies, dx, dz, *pieces):
         for p in pieces:
             copies[dz, p].wait_recv()
             to_sibling(dx, dz, p)
 
-    zx = {}
-
-    def relay(copies, dx, p):
-        dz = 1 if p in ("n0", "f0") else 3
-        copies[2, p] = send(f"z{dz}", part(gathered[dx, dz, 0], p), part(gathered[dx, 2, 0], p))
-
-    def near_z(copies, dx, p):
-        copies[1, p].wait_recv()
-        copies[3, p].wait_recv()
-        relay(copies, dx, p)
-        to_sibling(dx, 1, p)
-        to_sibling(dx, 3, p)
-
-    def x_after_z(dz, pieces):
+    def x_after_z(dz, *pieces):
         for p in pieces:
             zx[dz, p] = send("xi", part(gathered[0, dz, 0], p), part(gathered[1, dz, 0], p))
 
-    near_z(zo, 0, "f0")
     over_x("n0")
-    near_z(zo, 0, "f1")
-    x_after_z(1, F_PIECES)
-    x_after_z(3, F_PIECES)
+    near_z(zo, 0, "f", "f0", "f1")
+    x_after_z(1, "f")
+    x_after_z(3, "f")
     over_x("n1")
-    for p in N_PIECES:
-        for dz in (1, 3):
-            zx[dz, p] = send(f"z{dz}", part(gathered[1, 0, 0], p), part(gathered[1, dz, 0], p))
+    for dz in (1, 3):
+        zx[dz, "n"] = send(f"z{dz}", part(gathered[1, 0, 0], "n"), part(gathered[1, dz, 0], "n"))
+    to_sibling(1, 0, "n")
     arrived(sent_b[0, 2])
     beta_owner(0, 2)
-    near_z(zo, 0, "n0")
     over_x("f0")
     arrived([xo["n0"], xo["n1"]])
     by_column(peer[0], peer_cb[0], PARTS[0][1])
     stage_peer(0)
-    near_z(zo, 0, "n1")
+    send_peer(0)
+    near_z(zo, 0, "n", "n0", "n1")
     over_x("f1")
-    send_peer(0)
+    to_sibling(1, 0, "f")
     arrived(sent_b[0, 1])
     beta_owner(0, 1)
     arrived(sent_b[0, 3])
     beta_owner(0, 3)
-    from_z(zo, 0, 2, F_PIECES)
-    x_after_z(2, F_PIECES)
+    after(zo, 0, 2, "f0", "f1")
+    x_after_z(2, "fa", "fb")
     arrived([xo["f0"], xo["f1"]])
     by_column(peer[1], peer_cb[1], PARTS[1][1])
     stage_peer(1)
-    from_z(zx, 1, 1, F_PIECES)
+    after(zx, 1, 1, "f")
     arrived(sib[1, 0])
+    send_peer(1)
     alpha_chip(1, 0)
-    send_peer(1)
-    near_z(zx, 1, "n0")
     arrived(sib[0, 1])
     alpha_chip(0, 1)
     beta_owner(1, 0)
+    near_z(zx, 1, "n", "n0a", "n0b", "n1a", "n1b")
     arrived(sib[0, 3])
     alpha_chip(0, 3)
-    near_z(zx, 1, "n1")
     arrived(sib[1, 1])
     alpha_chip(1, 1)
-    from_z(zx, 1, 3, F_PIECES)
+    after(zx, 1, 3, "f")
     arrived(sent_b[1, 2])
     beta_owner(1, 2)
+    after(zo, 0, 2, "n0", "n1")
     arrived(sib[1, 3])
     alpha_chip(1, 3)
-    from_z(zo, 0, 2, N_PIECES)
-    from_z(zx, 1, 2, ("f0",))
+    arrived(sib[0, 2])
+    alpha_chip(0, 2)
     arrived(sent_b[1, 1])
     beta_owner(1, 1)
+    after(zx, 1, 2, "n0a", "n1a")
     arrived(sent_b[1, 3])
     beta_owner(1, 3)
-    arrived(sib[0, 2])
-    alpha_chip(0, 2)
     alpha_weights(1, 2)
-    from_z(zx, 1, 2, ("f1",) + N_PIECES)
+    after(zx, 1, 2, "n0b", "fa", "n1b", "fb")
     alpha_inputs(1, 2, 0)
     tiles(add_alpha_lane)
     arrived(sib[1, 2])

time: 68.1 us -> 67.9 us (level)
  no operation moved by 1% of the time
where the time goes in v4:
time: 67.9 us; the launch traced here: 67.8 us
  Pallas kernels  66.8 us (98%)
  local copies, waits for them, and re-layouts  0.97 us (1%)
    pallas_call x1, Pallas kernels, per_device(): pl.pallas_call(body, out_shape=pltpu.VMEM((ROWS, COLS), jnp.bfloat16), in...  66.8 us

profile of v4, /device:TPU:1, one launch (start us, length us, event | category | flops | bytes accessed | tf_op | source)
XLA Modules:
  0.0 67.8 jit_solution(17064195164061496415)
XLA Ops:
  0.0 66.8 %shard_map.64 = bf16[512,1024]{1,0:T(8,128)(2,1)S(1)} custom-call(s32[14,64]{1,0:T(8,128)} %bitcast.4, s32[14,64]{1,0:T(8,128)} %bitcast.5, bf16[32,16,1024]{2,1,0:T(8,128)(2,1)} %bitcast.3, f32[512,1024]{1,0:T(8,128)} %diag_hbm.1, bf16[4,14,128,128]{3,2,1,0:T(8,128)(2,1)} %ab_hbm.1, bf16[8,14,128,128]{3,2,1,0:T(8,128)(2,1)} %bb_hbm.1), custom_call_target="tpu_custom_call" | custom-call | tf_op jit(solution)/shard_map/pallas_call | solution.py:424
  66.8 1.0 %copy.8 = bf16[512,1024]{1,0:T(8,128)(2,1)} copy(bf16[512,1024]{1,0:T(8,128)(2,1)S(1)} %shard_map.64) | data formatting | bytes 2097152

commit v5 on v4

--- a/solution.py
+++ b/solution.py
@@ -18,28 +18,22 @@
 PER = BLK // 16
 
 PIECES = {
-    "n": (0, 17),
-    "n0": (0, 8),
-    "n1": (8, 9),
-    "n0a": (0, 5),
-    "n0b": (5, 3),
-    "n1a": (8, 6),
-    "n1b": (14, 3),
-    "f": (17, 15),
-    "f0": (17, 8),
+    "n": (0, 18),
+    "n0": (0, 9),
+    "n1": (9, 9),
+    "f": (18, 14),
+    "f0": (18, 7),
     "f1": (25, 7),
-    "fa": (17, 11),
-    "fb": (28, 4),
 }
 PARTS = (PIECES["n"], PIECES["f"])
 NSEM = 96
-COMPUTE = True
 
 INV_A = 0
 INV_B = 8
 SEL_A = 40
 SEL_B = 56
-TABLE = 88
+SEL_NEAR = {"xi": 88, "z1": 104, "z3": 120}
+TABLE = 136
 
 
 def body(la_hbm, lb_hbm, c_hbm, diag_hbm, ab_hbm, bb_hbm, out_ref, *scratch):
@@ -49,8 +43,10 @@
     for dx in range(2):
         for dz in range(4):
             for dc in range(2):
-                if (dx, dz, dc) != (0, 0, 0):
+                if (dx, dz, dc) != (0, 0, 0) and dz != 2:
                     gathered[dx, dz, dc] = next(it)
+    far = [[next(it) for _ in range(2)] for _ in range(2)]
+    leaf_z, leaf_x, pick_z, pick_x = ([next(it) for _ in range(2)] for _ in range(4))
     peer = [next(it), next(it)]
     peer_cb = [next(it), next(it)]
     message = {(q, dy): next(it) for q in range(2) for dy in (1, 2, 3)}
@@ -118,8 +114,8 @@
     for p in ("n0", "n1", "f0", "f1"):
         xi[p] = send("xi", part(c_hbm, p), part(gathered[1, 0, 0], p))
     zo = {}
-    for p in ("f", "n"):
-        for dz in (1, 3):
+    for dz, order in ((1, ("f", "n")), (3, ("n", "f"))):
+        for p in order:
             zo[dz, p] = send(f"z{dz}", part(c_hbm, p), part(gathered[0, dz, 0], p))
     sib[0, 0] = [send("s", c_hbm, gathered[0, 0, 1])]
 
@@ -153,12 +149,14 @@
     load_lb.wait()
     lists_a[...] = la[...].T
     lists_b[...] = lb[...].T
-    inv = slots_of(lists_a[pl.ds(pl.multiple_of((ia // 2) * 8, 8), 8), :])
-    table[INV_A : INV_A + 8, :] = inv
     row = lax.broadcasted_iota(jnp.int32, (8, BLK), 0)
-    mine = (row // RA == core) & (inv < SLOTS)
-    needed = jnp.broadcast_to(jnp.max(jnp.where(mine, 1, 0), axis=0, keepdims=True), (8, BLK))
-    picks_of(needed, RA, CAP_A, SEL_A)
+    for first_row, device in [(SEL_A, ia)] + [(SEL_NEAR[link], target[link][0]) for link in SEL_NEAR]:
+        inv = slots_of(lists_a[pl.ds(pl.multiple_of((device // 2) * 8, 8), 8), :])
+        if first_row == SEL_A:
+            table[INV_A : INV_A + 8, :] = inv
+        mine = (row // RA == core) & (inv < SLOTS)
+        needed = jnp.broadcast_to(jnp.max(jnp.where(mine, 1, 0), axis=0, keepdims=True), (8, BLK))
+        picks_of(needed, RA, CAP_A, first_row)
     needed = jnp.zeros((8, BLK), jnp.int32)
     for d in range(4):
         inv = slots_of(lists_b[pl.ds(pl.multiple_of(x_hi * 32 + d * 8, 8), 8), :])
@@ -221,45 +219,38 @@
     def alpha_inputs(dx, dz, *lanes):
         for dc in lanes:
             owner = alpha_at(dx, 4 - dz, dc)
-            source = own if (dx, dz, dc) == (0, 0, 0) else gathered[dx, dz, dc]
             for s in range(CAP_A):
-                first = (tab[SEL_A + 8 * s, owner * RA] % RA) * PER
+                block = tab[SEL_A + 8 * s, owner * RA] % RA
                 for t in range(PER):
                     at = (dc * CAP_A + s) * BLK + t * 16
-                    xa[at : at + 16, :] = source[first + t]
-
-    def tiles(one):
-        def tile(n, carry):
-            one(pl.ds(pl.multiple_of(n * 256, 256), 256))
-            return carry
-
-        lax.fori_loop(0, COLS // 256, tile, 0)
-
-    def alpha_dot(cols, *lanes):
+                    half, u = t // (PER // 2), t % (PER // 2)
+                    if (dx, dz) == (1, 2):
+                        rows = (leaf_z, leaf_x)[half][dc][s, u]
+                    elif dz == 2:
+                        rows = far[half][dc][block, u]
+                    else:
+                        source = own if (dx, dz, dc) == (0, 0, 0) else gathered[dx, dz, dc]
+                        rows = source[block * PER + t]
+                    xa[at : at + 16, :] = rows
+
+    def alpha_dot(*lanes):
         depth = pl.ds(lanes[0] * CAP_A * BLK, len(lanes) * CAP_A * BLK)
-        return jnp.dot(wa[:, depth], xa[depth, cols], preferred_element_type=jnp.float32)
-
-    def add_alpha(cols):
-        acc[:, cols] += alpha_dot(cols, 0, 1)
-
-    def add_alpha_lane(cols):
-        acc[:, cols] += alpha_dot(cols, 0)
-
-    def add_beta(cols):
-        acc[:, cols] += lax.dot_general(
-            xb[...], wb[cols, :], (((1,), (1,)), ((), ())), preferred_element_type=jnp.float32
+        return jnp.dot(wa[:, depth], xa[depth, :], preferred_element_type=jnp.float32)
+
+    def add_alpha(*lanes):
+        acc[...] += alpha_dot(*lanes)
+
+    def add_beta():
+        acc[...] += lax.dot_general(
+            xb[...], wb[...], (((1,), (1,)), ((), ())), preferred_element_type=jnp.float32
         )
 
     def alpha_chip(dx, dz):
-        if not COMPUTE:
-            return
         alpha_weights(dx, dz)
         alpha_inputs(dx, dz, 0, 1)
-        tiles(add_alpha)
+        add_alpha(0, 1)
 
     def beta_owner(q, dy):
-        if not COMPUTE:
-            return
         owner = beta_at(q, 4 - dy)
         for s in range(CAP_B):
             pick = tab[SEL_B + 8 * s + y, owner * RB]
@@ -273,7 +264,7 @@
                     xb[pl.ds(PARTS[h][0] * 16, PARTS[h][1] * 16), column] = peer_cb[h][pick % RB]
             else:
                 xb[:, column] = own_cb[pick % RB]
-        tiles(add_beta)
+        add_beta()
 
     def arrived(copies):
         for copy in copies:
@@ -303,33 +294,64 @@
         xi[p].wait_recv()
         xo[p] = send("xo", part(gathered[1, 0, 0], p), peer[h].at[pl.ds(first - PARTS[h][0], size)])
 
-    zx = {}
-
-    def relay(copies, dx, *pieces):
-        for p in pieces:
-            dz = 1 if p[:2] in ("n0", "f0") else 3
-            copies[2, p] = send(f"z{dz}", part(gathered[dx, dz, 0], p), part(gathered[dx, 2, 0], p))
-
-    def near_z(copies, dx, p, *halves):
-        for dz in (1, 3):
-            copies[dz, p].wait_recv()
-        relay(copies, dx, *halves)
-        for dz in (1, 3):
-            to_sibling(dx, dz, p)
+    zx, zfar, xleaf, zleaf = {}, {}, {}, {}
+
+    def relay(half):
+        for i in range(2):
+            for dz, block in ((1, 2 + i), (3, i)):
+                rows = gathered[0, dz, 0].at[pl.ds(block * PER + half * (PER // 2), PER // 2)]
+                zfar[half, block] = send(f"z{dz}", rows, far[half][0].at[block])
+
+    def far_to_sibling(half):
+        for block in (2, 0, 3, 1):
+            zfar[half, block].wait_recv()
+            copy = send("s", far[half][0].at[block], far[half][1].at[block])
+            sib.setdefault((0, 2, half), []).append(copy)
 
     def after(copies, dx, dz, *pieces):
         for p in pieces:
             copies[dz, p].wait_recv()
             to_sibling(dx, dz, p)
 
-    def x_after_z(dz, *pieces):
-        for p in pieces:
-            zx[dz, p] = send("xi", part(gathered[0, dz, 0], p), part(gathered[1, dz, 0], p))
+    def x_after_z(dz, p):
+        zx[dz, p] = send("xi", part(gathered[0, dz, 0], p), part(gathered[1, dz, 0], p))
+
+    def picked_for(link, s, dx, dz, dc):
+        return tab[SEL_NEAR[link] + 8 * s, alpha_at(dx, 4 - dz, dc) * RA] % RA
+
+    def stage_x():
+        for dc in range(2):
+            for s in range(CAP_A):
+                block = picked_for("xi", s, 0, 2, dc)
+                for t in range(PER // 2):
+                    pick_x[dc][s, t] = far[1][dc][block, t]
+
+    def send_x():
+        for dc in range(2):
+            xleaf[dc] = send("xi", pick_x[dc], leaf_x[dc])
+
+    def stage_z():
+        for dc, dz in enumerate((1, 3)):
+            for s in range(CAP_A):
+                first = picked_for(f"z{dz}", s, 1, dz, dc) * PER
+                for t in range(PER // 2):
+                    pick_z[dc][s, t] = gathered[1, dz, dc][first + t]
+
+    def send_z():
+        for dc, dz in enumerate((1, 3)):
+            zleaf[dc] = send(f"z{dz}", pick_z[dc], leaf_z[dc])
+
+    def over_x(p):
+        h = int(p in ("f0", "f1"))
+        first, size = PIECES[p]
+        xi[p].wait_recv()
+        xo[p] = send("xo", part(gathered[1, 0, 0], p), peer[h].at[pl.ds(first - PARTS[h][0], size)])
 
     over_x("n0")
-    near_z(zo, 0, "f", "f0", "f1")
-    x_after_z(1, "f")
-    x_after_z(3, "f")
+    after(zo, 0, 1, "f")
+    x_after_z(1, "f0")
+    after(zo, 0, 3, "n")
+    relay(1)
     over_x("n1")
     for dz in (1, 3):
         zx[dz, "n"] = send(f"z{dz}", part(gathered[1, 0, 0], "n"), part(gathered[1, dz, 0], "n"))
@@ -341,56 +363,60 @@
     by_column(peer[0], peer_cb[0], PARTS[0][1])
     stage_peer(0)
     send_peer(0)
-    near_z(zo, 0, "n", "n0", "n1")
+    after(zo, 0, 3, "f")
+    x_after_z(3, "f")
+    x_after_z(1, "f1")
+    after(zo, 0, 1, "n")
+    relay(0)
     over_x("f1")
     to_sibling(1, 0, "f")
     arrived(sent_b[0, 1])
     beta_owner(0, 1)
     arrived(sent_b[0, 3])
     beta_owner(0, 3)
-    after(zo, 0, 2, "f0", "f1")
-    x_after_z(2, "fa", "fb")
+    far_to_sibling(1)
+    after(zx, 1, 1, "f0")
     arrived([xo["f0"], xo["f1"]])
     by_column(peer[1], peer_cb[1], PARTS[1][1])
     stage_peer(1)
-    after(zx, 1, 1, "f")
+    arrived(sib[0, 2, 1])
+    send_peer(1)
+    stage_x()
     arrived(sib[1, 0])
-    send_peer(1)
     alpha_chip(1, 0)
+    send_x()
     arrived(sib[0, 1])
     alpha_chip(0, 1)
     beta_owner(1, 0)
-    near_z(zx, 1, "n", "n0a", "n0b", "n1a", "n1b")
     arrived(sib[0, 3])
     alpha_chip(0, 3)
+    after(zx, 1, 3, "f", "n")
+    after(zx, 1, 1, "n", "f1")
+    arrived(sib[1, 3])
+    stage_z()
     arrived(sib[1, 1])
-    alpha_chip(1, 1)
-    after(zx, 1, 3, "f")
+    alpha_weights(1, 1)
+    alpha_inputs(1, 1, 0, 1)
+    send_z()
+    add_alpha(0, 1)
+    alpha_chip(1, 3)
+    far_to_sibling(0)
+    arrived(sib[0, 2, 0])
+    alpha_chip(0, 2)
     arrived(sent_b[1, 2])
     beta_owner(1, 2)
-    after(zo, 0, 2, "n0", "n1")
-    arrived(sib[1, 3])
-    alpha_chip(1, 3)
-    arrived(sib[0, 2])
-    alpha_chip(0, 2)
     arrived(sent_b[1, 1])
     beta_owner(1, 1)
-    after(zx, 1, 2, "n0a", "n1a")
     arrived(sent_b[1, 3])
     beta_owner(1, 3)
     alpha_weights(1, 2)
-    after(zx, 1, 2, "n0b", "fa", "n1b", "fb")
+    arrived([zleaf[0], zleaf[1], xleaf[0]])
     alpha_inputs(1, 2, 0)
-    tiles(add_alpha_lane)
-    arrived(sib[1, 2])
+    add_alpha(0)
+    arrived([xleaf[1]])
     alpha_inputs(1, 2, 1)
 
-    def last(n, carry):
-        cols = pl.ds(pl.multiple_of(n * 256, 256), 256)
-        out_ref[:, cols] = (acc[:, cols] + alpha_dot(cols, 1)).astype(jnp.bfloat16)
-        return carry
-
-    lax.fori_loop(0, COLS // 256, last, 0)
+    out_ref[...] = (acc[...] + alpha_dot(1)).astype(jnp.bfloat16)
     for copy in started:
         copy.wait_send()
     assert len(started) <= NSEM, len(started)
@@ -398,9 +424,11 @@
 
 def per_device(coefficients, diagonal, alpha_blocks, alpha_lists, beta_blocks, beta_lists):
     grouped = pltpu.VMEM((GROUPS, 16, COLS), jnp.bfloat16)
+    halves = pltpu.VMEM((RA, PER // 2, 16, COLS), jnp.bfloat16)
+    picked = pltpu.VMEM((CAP_A, PER // 2, 16, COLS), jnp.bfloat16)
     by_block = pltpu.VMEM((RB, ROWS, BLK), jnp.bfloat16)
     slots = pltpu.VMEM((CAP_B, ROWS, BLK), jnp.bfloat16)
-    scratch = [grouped, by_block] + [grouped] * 15 + [pltpu.VMEM((n, 16, COLS), jnp.bfloat16) for _, n in PARTS]
+    scratch = [grouped, by_block] + [grouped] * 11 + [halves] * 4 + [picked] * 8 + [pltpu.VMEM((n, 16, COLS), jnp.bfloat16) for _, n in PARTS]
     scratch += [pltpu.VMEM((RB, n * 16, BLK), jnp.bfloat16) for _, n in PARTS] + [slots] * 12
     scratch += [
         pltpu.VMEM((SLOTS, 64), jnp.int32),

time: 67.9 us -> 64.6 us (0.951)
  Pallas kernels: 66.8 us -> 63.5 us
    pallas_call x1, Pallas kernels: 66.8 us -> 63.5 us  [per_device(): pl.pallas_call(body, out_shape=pltpu.VMEM((ROWS, COLS), jnp.bfloat16), in...]
where the time goes in v5:
time: 64.6 us; the launch traced here: 64.5 us
  Pallas kernels  63.5 us (98%)
  local copies, waits for them, and re-layouts  0.97 us (2%)
    pallas_call x1, Pallas kernels, per_device(): pl.pallas_call(body, out_shape=pltpu.VMEM((ROWS, COLS), jnp.bfloat16), in...  63.5 us

profile of v5, /device:TPU:1, one launch (start us, length us, event | category | flops | bytes accessed | tf_op | source)
XLA Modules:
  0.0 64.5 jit_solution(11568379700358168404)
XLA Ops:
  0.0 63.5 %shard_map.64 = bf16[512,1024]{1,0:T(8,128)(2,1)S(1)} custom-call(s32[14,64]{1,0:T(8,128)} %bitcast.4, s32[14,64]{1,0:T(8,128)} %bitcast.5, bf16[32,16,1024]{2,1,0:T(8,128)(2,1)} %bitcast.3, f32[512,1024]{1,0:T(8,128)} %diag_hbm.1, bf16[4,14,128,128]{3,2,1,0:T(8,128)(2,1)} %ab_hbm.1, bf16[8,14,128,128]{3,2,1,0:T(8,128)(2,1)} %bb_hbm.1), custom_call_target="tpu_custom_call" | custom-call | tf_op jit(solution)/shard_map/pallas_call | solution.py:452
  63.6 1.0 %copy.8 = bf16[512,1024]{1,0:T(8,128)(2,1)} copy(bf16[512,1024]{1,0:T(8,128)(2,1)S(1)} %shard_map.64) | data formatting | bytes 2097152

commit v6 on v5

--- a/solution.py
+++ b/solution.py
@@ -330,16 +330,15 @@
         for dc in range(2):
             xleaf[dc] = send("xi", pick_x[dc], leaf_x[dc])
 
-    def stage_z():
-        for dc, dz in enumerate((1, 3)):
-            for s in range(CAP_A):
-                first = picked_for(f"z{dz}", s, 1, dz, dc) * PER
-                for t in range(PER // 2):
-                    pick_z[dc][s, t] = gathered[1, dz, dc][first + t]
-
-    def send_z():
-        for dc, dz in enumerate((1, 3)):
-            zleaf[dc] = send(f"z{dz}", pick_z[dc], leaf_z[dc])
+    def stage_z(dc):
+        dz = (1, 3)[dc]
+        for s in range(CAP_A):
+            first = picked_for(f"z{dz}", s, 1, dz, dc) * PER
+            for t in range(PER // 2):
+                pick_z[dc][s, t] = gathered[1, dz, dc][first + t]
+
+    def send_z(dc):
+        zleaf[dc] = send(f"z{(1, 3)[dc]}", pick_z[dc], leaf_z[dc])
 
     def over_x(p):
         h = int(p in ("f0", "f1"))
@@ -391,15 +390,20 @@
     arrived(sib[0, 3])
     alpha_chip(0, 3)
     after(zx, 1, 3, "f", "n")
-    after(zx, 1, 1, "n", "f1")
+    after(zx, 1, 1, "n")
     arrived(sib[1, 3])
-    stage_z()
+    stage_z(1)
+    alpha_weights(1, 3)
+    send_z(1)
+    alpha_inputs(1, 3, 0, 1)
+    add_alpha(0, 1)
+    after(zx, 1, 1, "f1")
+    stage_z(0)
+    alpha_weights(1, 1)
+    send_z(0)
     arrived(sib[1, 1])
-    alpha_weights(1, 1)
     alpha_inputs(1, 1, 0, 1)
-    send_z()
     add_alpha(0, 1)
-    alpha_chip(1, 3)
     far_to_sibling(0)
     arrived(sib[0, 2, 0])
     alpha_chip(0, 2)
@@ -410,10 +414,10 @@
     arrived(sent_b[1, 3])
     beta_owner(1, 3)
     alpha_weights(1, 2)
-    arrived([zleaf[0], zleaf[1], xleaf[0]])
+    arrived([zleaf[0], xleaf[0]])
     alpha_inputs(1, 2, 0)
     add_alpha(0)
-    arrived([xleaf[1]])
+    arrived([zleaf[1], xleaf[1]])
     alpha_inputs(1, 2, 1)
 
     out_ref[...] = (acc[...] + alpha_dot(1)).astype(jnp.bfloat16)

time: 64.6 us -> 64.2 us (level)
  no operation moved by 1% of the time
where the time goes in v6:
time: 64.2 us; the launch traced here: 64.1 us
  Pallas kernels  63.2 us (98%)
  local copies, waits for them, and re-layouts  0.97 us (2%)
    pallas_call x1, Pallas kernels, per_device(): pl.pallas_call(body, out_shape=pltpu.VMEM((ROWS, COLS), jnp.bfloat16), in...  63.2 us

profile of v6, /device:TPU:1, one launch (start us, length us, event | category | flops | bytes accessed | tf_op | source)
XLA Modules:
  0.0 64.1 jit_solution(13210978576607099192)
XLA Ops:
  0.0 63.2 %shard_map.64 = bf16[512,1024]{1,0:T(8,128)(2,1)S(1)} custom-call(s32[14,64]{1,0:T(8,128)} %bitcast.4, s32[14,64]{1,0:T(8,128)} %bitcast.5, bf16[32,16,1024]{2,1,0:T(8,128)(2,1)} %bitcast.3, f32[512,1024]{1,0:T(8,128)} %diag_hbm.1, bf16[4,14,128,128]{3,2,1,0:T(8,128)(2,1)} %ab_hbm.1, bf16[8,14,128,128]{3,2,1,0:T(8,128)(2,1)} %bb_hbm.1), custom_call_target="tpu_custom_call" | custom-call | tf_op jit(solution)/shard_map/pallas_call | solution.py:456
  63.2 1.0 %copy.8 = bf16[512,1024]{1,0:T(8,128)(2,1)} copy(bf16[512,1024]{1,0:T(8,128)(2,1)S(1)} %shard_map.64) | data formatting | bytes 2097152

commit v7 on v6

--- a/solution.py
+++ b/solution.py
@@ -175,11 +175,9 @@
 
     for r in range(RA):
         ablk[r, SLOTS] = jnp.zeros((BLK, BLK), jnp.bfloat16)
-    for r in range(RB):
-        bblk[r, SLOTS] = jnp.zeros((BLK, BLK), jnp.bfloat16)
     load_own.wait()
+    by_column(own, own_cb, GROUPS)
     load_tab = local(6, table, tab)
-    by_column(own, own_cb, GROUPS)
     load_tab.wait()
 
     def pick_b(d, q, s):
@@ -271,6 +269,8 @@
             copy.wait_recv()
 
     stage_own()
+    for r in range(RB):
+        bblk[r, SLOTS] = jnp.zeros((BLK, BLK), jnp.bfloat16)
     send_own()
     load_d.wait()
 
@@ -355,12 +355,12 @@
     for dz in (1, 3):
         zx[dz, "n"] = send(f"z{dz}", part(gathered[1, 0, 0], "n"), part(gathered[1, dz, 0], "n"))
     to_sibling(1, 0, "n")
-    arrived(sent_b[0, 2])
-    beta_owner(0, 2)
     over_x("f0")
     arrived([xo["n0"], xo["n1"]])
     by_column(peer[0], peer_cb[0], PARTS[0][1])
     stage_peer(0)
+    arrived(sent_b[0, 2])
+    beta_owner(0, 2)
     send_peer(0)
     after(zo, 0, 3, "f")
     x_after_z(3, "f")
@@ -379,8 +379,8 @@
     by_column(peer[1], peer_cb[1], PARTS[1][1])
     stage_peer(1)
     arrived(sib[0, 2, 1])
+    stage_x()
     send_peer(1)
-    stage_x()
     arrived(sib[1, 0])
     alpha_chip(1, 0)
     send_x()

time: 64.2 us -> 64.2 us (level)
  no operation moved by 1% of the time
where the time goes in v7:
time: 64.2 us; the launch traced here: 64.1 us
  Pallas kernels  63.2 us (98%)
  local copies, waits for them, and re-layouts  0.97 us (2%)
    pallas_call x1, Pallas kernels, per_device(): pl.pallas_call(body, out_shape=pltpu.VMEM((ROWS, COLS), jnp.bfloat16), in...  63.2 us

profile of v7, /device:TPU:1, one launch (start us, length us, event | category | flops | bytes accessed | tf_op | source)
XLA Modules:
  0.0 64.1 jit_solution(805446399784511748)
XLA Ops:
  0.0 63.2 %shard_map.64 = bf16[512,1024]{1,0:T(8,128)(2,1)S(1)} custom-call(s32[14,64]{1,0:T(8,128)} %bitcast.4, s32[14,64]{1,0:T(8,128)} %bitcast.5, bf16[32,16,1024]{2,1,0:T(8,128)(2,1)} %bitcast.3, f32[512,1024]{1,0:T(8,128)} %diag_hbm.1, bf16[4,14,128,128]{3,2,1,0:T(8,128)(2,1)} %ab_hbm.1, bf16[8,14,128,128]{3,2,1,0:T(8,128)(2,1)} %bb_hbm.1), custom_call_target="tpu_custom_call" | custom-call | tf_op jit(solution)/shard_map/pallas_call | solution.py:456
  63.2 1.0 %copy.8 = bf16[512,1024]{1,0:T(8,128)(2,1)} copy(bf16[512,1024]{1,0:T(8,128)(2,1)S(1)} %shard_map.64) | data formatting | bytes 2097152
